TPU v7x, 256 devices: a whole 4x4x8 slice. The times are simulated.
256 devices in a mesh: scan: 16 (over y, x), blk: 16 (over z, core).
Axes of the slice: x: 4, y: 4, z: 8, core: 2. Of those that a mesh axis runs over, the one named last changes fastest.
Arguments:
- ref_feats: bfloat16 [16, 8192, 256], P('scan', 'blk'), may hold values from -120 to 120
- src_feats: bfloat16 [16, 2048, 256], P('scan', 'blk'), may hold values from -120 to 120
- grad_out: bfloat16 [16, 8192, 256], P('scan', 'blk'), may hold values from -6 to 6
- w_query: bfloat16 [256, 256], replicated, may hold values from -1 to 1
- w_key: bfloat16 [256, 256], replicated, may hold values from -1 to 1
- w_value: bfloat16 [256, 256], replicated, may hold values from -0.375 to 0.375
- w_out: bfloat16 [256, 256], replicated, may hold values from -0.375 to 0.375
- intersection: int32 [16, 64, 16], P('scan', 'blk'), may hold values from 0 to 1, as said below
Outputs:
- matched: bfloat16 [16, 8192, 256], P('scan', 'blk')
- grad_ref: bfloat16 [16, 8192, 256], P('scan', 'blk')
- grad_src: bfloat16 [16, 2048, 256], P('scan', 'blk')
- grad_w_query: float32 [256, 256], replicated
- grad_w_key: float32 [256, 256], replicated
- grad_w_value: float32 [256, 256], replicated
- grad_w_out: float32 [256, 256], replicated
Inputs may be any that keep to these rules, and one draw needn't show every extreme that they name: intersection[p, b, c] is 1 for c = b * 16 // 64, so every reference block and every source block of a pair has a listed partner.
All inputs are finite; a program needn't handle non-finite values.
Results may differ from a plain program's by a relative error of at most 0.035.
Values may be sent and summed in bfloat16 or wider, within the bound.
A program may use at most 64 MiB of HBM per device.

v0:
```python
import math

import jax
import jax.numpy as jnp
from jax import lax
from jax.sharding import PartitionSpec as P

HEADS = 4
BLOCK = 128


NEG = -1e30


def combined_all(part, axis, combine):
    gathered = jax.tree.map(lambda a: lax.all_gather(a, axis), part)

    def take(source):
        return jax.tree.map(lambda a: lax.dynamic_index_in_dim(a, source, 0, False), gathered)

    return lax.fori_loop(
        1, lax.axis_size(axis), lambda source, state: combine(state, take(source)), take(0)
    )


def combine_stats(first_stats, second_stats):
    peak_now = jnp.maximum(first_stats[0], second_stats[0])
    total_now = first_stats[1] * jnp.exp(first_stats[0] - peak_now) + second_stats[1] * jnp.exp(
        second_stats[0] - peak_now
    )
    return (peak_now, total_now)


def exact_dot(left, right):
    return jnp.dot(left, right, precision=lax.Precision.HIGHEST)


def on_device(ref_feats, src_feats, grad_out, w_query, w_key, w_value, w_out, intersection):
    ref_rows = ref_feats[0]
    src_rows = src_feats[0]
    out_grad = grad_out[0]
    blocks = intersection[0] == 1
    query_count = ref_rows.shape[0]
    model_width = ref_rows.shape[1]
    head_count = HEADS
    head_dim = model_width // head_count
    score_scale = head_dim ** (-0.5)
    queries = jnp.dot(ref_rows, w_query, preferred_element_type=jnp.float32).astype(jnp.bfloat16)
    query_heads = queries.reshape(query_count, head_count, head_dim)
    grad_att = jnp.dot(out_grad, w_out.T, preferred_element_type=jnp.float32).astype(jnp.bfloat16)
    grad_heads = grad_att.reshape(query_count, head_count, head_dim)
    key_local = jnp.dot(src_rows, w_key, preferred_element_type=jnp.float32).astype(jnp.bfloat16)
    value_local = jnp.dot(src_rows, w_value, preferred_element_type=jnp.float32).astype(
        jnp.bfloat16
    )
    joined = lax.all_gather(
        jnp.concatenate([key_local, value_local], axis=1), "blk", axis=0, tiled=True
    )
    keys_all = joined[:, :model_width]
    values_all = joined[:, model_width:]
    key_total = keys_all.shape[0]

    def mask_blocks(first_row, tile_rows):
        return lax.dynamic_slice_in_dim(blocks, first_row // BLOCK, tile_rows // BLOCK, 1)

    def allowed_at(first_row, tile_rows):
        mask_piece = mask_blocks(first_row, tile_rows)
        mask_wide = jnp.broadcast_to(
            mask_piece[:, None, :, None], (mask_piece.shape[0], BLOCK, mask_piece.shape[1], BLOCK)
        )
        return mask_wide.reshape(query_count, tile_rows)[None]

    def key_heads(first_row, tile_rows):
        return lax.dynamic_slice_in_dim(keys_all, first_row, tile_rows, 0).reshape(
            tile_rows, head_count, head_dim
        )

    def value_heads(first_row, tile_rows):
        return lax.dynamic_slice_in_dim(values_all, first_row, tile_rows, 0).reshape(
            tile_rows, head_count, head_dim
        )

    def raw_scores(first_row, tile_rows):
        return (
            jnp.einsum(
                "ihc,jhc->hij",
                query_heads,
                key_heads(first_row, tile_rows),
                preferred_element_type=jnp.float32,
            )
            * score_scale
        )

    def sweep(update, carried, first_row, row_count):
        tile_rows = math.gcd(4 * BLOCK, row_count)

        def visit_tile(tile_index, state_now):
            tile_first = first_row + tile_index * tile_rows
            return update(state_now, tile_first, tile_rows)

        return lax.fori_loop(0, row_count // tile_rows, visit_tile, carried)

    def stats_update(state_now, first_row, tile_rows):
        row_peak, row_total, col_peak, col_total = state_now
        allowed = allowed_at(first_row, tile_rows)
        scores = raw_scores(first_row, tile_rows)
        masked = jnp.where(allowed, scores, NEG)
        peak_next = jnp.maximum(row_peak, masked.max(axis=2))
        row_total = row_total * jnp.exp(row_peak - peak_next) + jnp.where(
            allowed, jnp.exp(scores - peak_next[:, :, None]), 0.0
        ).sum(axis=2)
        tile_peak = masked.max(axis=1)
        tile_total = jnp.where(allowed, jnp.exp(scores - tile_peak[:, None, :]), 0.0).sum(axis=1)
        col_peak = lax.dynamic_update_slice_in_dim(col_peak, tile_peak, first_row, 1)
        col_total = lax.dynamic_update_slice_in_dim(col_total, tile_total, first_row, 1)
        return (peak_next, row_total, col_peak, col_total)

    row_start = jnp.full((head_count, query_count), NEG, jnp.float32)
    col_start = jnp.full((head_count, key_total), NEG, jnp.float32)
    row_peak, row_total, col_peak, col_total = sweep(
        stats_update,
        (row_start, jnp.zeros_like(row_start), col_start, jnp.zeros_like(col_start)),
        0,
        key_total,
    )
    col_peak, col_total = combined_all((col_peak, col_total), "blk", combine_stats)

    def probabilities(first_row, tile_rows):
        allowed = allowed_at(first_row, tile_rows)
        scores = raw_scores(first_row, tile_rows)
        peak_piece = lax.dynamic_slice_in_dim(col_peak, first_row, tile_rows, 1)
        total_piece = lax.dynamic_slice_in_dim(col_total, first_row, tile_rows, 1)
        row_prob = (
            jnp.where(allowed, jnp.exp(scores - row_peak[:, :, None]), 0.0) / row_total[:, :, None]
        )
        col_prob = (
            jnp.where(allowed, jnp.exp(scores - peak_piece[:, None, :]), 0.0)
            / total_piece[:, None, :]
        )
        return (row_prob, col_prob, (row_prob * col_prob).astype(jnp.bfloat16))

    def forward_update(state_now, first_row, tile_rows):
        attended, row_dot, col_dot = state_now
        row_prob, col_prob, match_prob = probabilities(first_row, tile_rows)
        value_piece = value_heads(first_row, tile_rows)
        attended = attended + jnp.einsum(
            "hij,jhc->ihc", match_prob, value_piece, preferred_element_type=jnp.float32
        )
        grad_prob = jnp.einsum(
            "ihc,jhc->hij", grad_heads, value_piece, preferred_element_type=jnp.float32
        )
        product = match_prob.astype(jnp.float32) * grad_prob
        row_dot = row_dot + product.sum(axis=2)
        col_dot = lax.dynamic_update_slice_in_dim(col_dot, product.sum(axis=1), first_row, 1)
        return (attended, row_dot, col_dot)

    attended, row_dot, col_dot = sweep(
        forward_update,
        (
            jnp.zeros((query_count, head_count, head_dim), jnp.float32),
            jnp.zeros((head_count, query_count), jnp.float32),
            jnp.zeros((head_count, key_total), jnp.float32),
        ),
        0,
        key_total,
    )
    attended_rows = attended.reshape(query_count, model_width).astype(jnp.bfloat16)
    matched = (
        ref_rows.astype(jnp.float32)
        + jnp.dot(attended_rows, w_out, preferred_element_type=jnp.float32)
    ).astype(jnp.bfloat16)
    col_dot = lax.psum(col_dot, "blk")

    def score_grads(first_row, tile_rows):
        row_prob, col_prob, match_prob = probabilities(first_row, tile_rows)
        grad_prob = jnp.einsum(
            "ihc,jhc->hij",
            grad_heads,
            value_heads(first_row, tile_rows),
            preferred_element_type=jnp.float32,
        )
        column_share = lax.dynamic_slice_in_dim(col_dot, first_row, tile_rows, 1)
        grad_score = score_scale * (
            2.0 * match_prob.astype(jnp.float32) * grad_prob
            - row_prob * row_dot[:, :, None]
            - col_prob * column_share[:, None, :]
        )
        return (match_prob, grad_score.astype(jnp.bfloat16))

    def tile_grads(grad_acc, first_row, tile_rows):
        match_prob, grad_score = score_grads(first_row, tile_rows)
        grad_acc = grad_acc + jnp.einsum(
            "hij,jhc->ihc",
            grad_score,
            key_heads(first_row, tile_rows),
            preferred_element_type=jnp.float32,
        )
        grad_keys = jnp.einsum(
            "hij,ihc->jhc", grad_score, query_heads, preferred_element_type=jnp.float32
        )
        grad_values = jnp.einsum(
            "hij,ihc->jhc", match_prob, grad_heads, preferred_element_type=jnp.float32
        )
        return (
            grad_acc,
            grad_keys.reshape(tile_rows, model_width),
            grad_values.reshape(tile_rows, model_width),
        )

    query_start = jnp.zeros((query_count, head_count, head_dim), jnp.float32)

    def buffer_update(state_now, first_row, tile_rows):
        grad_acc, grad_keys, grad_values = tile_grads(state_now[0], first_row, tile_rows)
        buffer_now = lax.dynamic_update_slice_in_dim(
            state_now[1], jnp.concatenate([grad_keys, grad_values], axis=1), first_row, 0
        )
        return (grad_acc, buffer_now)

    grad_query, key_buffer = sweep(
        buffer_update,
        (query_start, jnp.zeros((key_total, 2 * model_width), jnp.float32)),
        0,
        key_total,
    )
    summed = lax.psum_scatter(
        key_buffer.astype(jnp.bfloat16), "blk", scatter_dimension=0, tiled=True
    ).astype(jnp.float32)
    grad_keys = summed[:, :model_width]
    grad_values = summed[:, model_width:]
    grad_src = (
        exact_dot(grad_keys, w_key.T.astype(jnp.float32))
        + exact_dot(grad_values, w_value.T.astype(jnp.float32))
    ).astype(jnp.bfloat16)
    source_wide = src_rows.astype(jnp.float32)
    weight_key = exact_dot(source_wide.T, grad_keys)
    weight_value = exact_dot(source_wide.T, grad_values)
    grad_query = grad_query.reshape(query_count, model_width).astype(jnp.bfloat16)
    grad_ref = (
        out_grad.astype(jnp.float32)
        + jnp.dot(grad_query, w_query.T, preferred_element_type=jnp.float32)
    ).astype(jnp.bfloat16)
    weight_query = jnp.einsum("ic,id->cd", ref_rows, grad_query, preferred_element_type=jnp.float32)
    weight_out = jnp.einsum(
        "ic,id->cd", attended_rows, out_grad, preferred_element_type=jnp.float32
    )
    weight_totals = lax.psum((weight_query, weight_key, weight_value, weight_out), ("scan", "blk"))
    return (
        matched[None],
        grad_ref[None],
        grad_src[None],
        weight_totals[0],
        weight_totals[1],
        weight_totals[2],
        weight_totals[3],
    )


def solution(mesh):
    in_specs = (
        P("scan", "blk", None),
        P("scan", "blk", None),
        P("scan", "blk", None),
        P(),
        P(),
        P(),
        P(),
        P("scan", "blk", None),
    )
    out_specs = (
        P("scan", "blk", None),
        P("scan", "blk", None),
        P("scan", "blk", None),
        P(),
        P(),
        P(),
        P(),
    )
    return jax.shard_map(
        on_device, mesh=mesh, in_specs=in_specs, out_specs=out_specs, check_vma=False
    )
```

profile of v0, /device:TPU:1, one launch (start us, length us, event | category | flops | bytes accessed | tf_op | source)
XLA Modules:
  0.0 643.6 jit_solution(6146754450756407287)
XLA Ops:
  12.8 1.9 convolution_convert_fusion
  14.8 39.3 %all-gather.6.cloned.1.call-done = bf16[2048,512]{1,0:T(8,128)(2,1)} async-done(((bf16[128,512]{1,0:T(8,128)(2,1)}), bf16[2048,512]{1,0:T(8,128)(2,1)}) %all-gather.6.cloned.1.call-update) | async-done | bytes 2097168 | tf_op jit(solution)/shard_map/all_gather | solution.py:56
  54.0 1.7 fusion.50
  55.7 1.4 copy.40
  57.2 35.2 %while.78 = (s32[]{:T(128)}, f32[4,512]{1,0:T(4,128)S(1)}, f32[4,512]{1,0:T(4,128)S(1)}, f32[4,2048]{1,0:T(4,128)S(1)}, f32[4,2048]{1,0:T(4,128)S(1)}, /*index=5...) while((s32[]{:T(128)}, f32[4,512]{1,0:T(4,128)S(1)}, ...), condition=%wide.region_5.6_spmd.clone, body=%wide.region_0.5_spmd.clone.sunk | while | flops 145758224 | bytes 10912189 | solution.py:101
  59.3 2.9 fusion.114
  62.2 3.8 fusion.115
  68.1 2.9 fusion.114
  71.0 3.8 fusion.115
  76.9 2.9 fusion.114
  79.8 3.8 fusion.115
  85.7 2.9 fusion.114
  88.6 3.8 fusion.115
  92.4 17.2 %all-gather.3 = f32[16,4,2048]{2,1,0:T(4,128)S(1)} all-gather(f32[1,4,2048]{2,1,0:T(4,128)S(1)} %bitcast.303), channel_id=3, replica_groups=mesh['scan'=16,'blk'=16] {'blk'}, dimensions={0}, use_global_device_ids=true | all-gather | bytes 557056 | tf_op jit(solution)/shard_map/all_gather | solution.py:16
  110.2 16.1 %all-gather.2 = f32[16,4,2048]{2,1,0:T(4,128)S(1)} all-gather(f32[1,4,2048]{2,1,0:T(4,128)S(1)} %bitcast.304), channel_id=2, replica_groups=mesh['scan'=16,'blk'=16] {'blk'}, dimensions={0}, use_global_device_ids=true | all-gather | bytes 557056 | tf_op jit(solution)/shard_map/all_gather | solution.py:16
  126.9 21.3 %while.77 = (s32[]{:T(128)}, f32[4,2048]{1,0:T(4,128)}, f32[4,2048]{1,0:T(4,128)}, f32[16,4,2048]{2,1,0:T(4,128)S(1)}, f32[16,4,2048]{2,1,0:T(4,128)S(1)}, /*index=5*/s32[]{:T(128)}, s32[]{:T(128)}, s32[]{:T(128)}) while((s32[]{:T(128)}, f32[4,2048]{1,0:T(4,128)}, f32[4,2048]{1,0:T(4,128)}, f32[16,4,2048]{2,1,0:T(4,128)S(1)}, ...), condition=%wide.region_7.8_spmd, body=%wide.region_6.7_spmd.sunk | while | flops 49157 | bytes 196739 | solution.py:21
  126.9 1.4 fusion.111
  128.3 1.4 fusion.111
  129.7 1.4 fusion.111
  131.1 1.4 fusion.111
  132.6 1.4 fusion.111
  134.0 1.4 fusion.111
  135.4 1.4 fusion.111
  136.8 1.4 fusion.111
  138.3 1.4 fusion.111
  139.7 1.4 fusion.111
  141.1 1.4 fusion.111
  142.5 1.4 fusion.111
  143.9 1.4 fusion.111
  145.4 1.4 fusion.111
  148.2 1.4 copy.38
  149.6 47.7 %while.79 = (s32[]{:T(128)}, f32[512,4,64]{0,2,1:T(8,128)}, f32[4,512]{1,0:T(4,128)}, f32[4,2048]{1,0:T(4,128)S(1)}, bf16[2048,256]{0,1:T(8,128)(2,1)}, /*index=...) while((s32[]{:T(128)}, f32[512,4,64]{0,2,1:T(8,128)}, ...), condition=%wide.region_11.12_spmd.clone, body=%wide.region_8.11_spmd.clone.sunk | while | flops 416546816 | bytes 10871277 | solution.py:101
  153.1 2.5 fusion.123
  156.5 1.9 fusion.125
  163.7 2.5 fusion.123
  167.1 1.9 fusion.125
  170.3 2.3 fusion.124
  176.0 2.5 fusion.123
  179.5 1.9 fusion.125
  182.7 2.3 fusion.124
  188.4 2.5 fusion.123
  191.9 1.9 fusion.125
  195.0 2.3 fusion.124
  197.3 44.0 %psum.35 = f32[4,2048]{1,0:T(4,128)} all-reduce(f32[4,2048]{1,0:T(4,128)S(1)} %get-tuple-element.993), channel_id=1, replica_groups=mesh['scan'=16,'blk'=16] {'blk'}, use_global_device_ids=true, to_apply=%region_12.13 | all-reduce | flops 8192 | bytes 65536 | tf_op jit(solution)/shard_map/psum | solution.py:172
  241.4 1.6 broadcast_in_dim.242
  243.0 56.8 %while.80 = (s32[]{:T(128)}, f32[512,4,64]{0,2,1:T(8,128)S(1)}, bf16[2048,512]{0,1:T(8,128)(2,1)}, bf16[2048,256]{0,1:T(8,128)(2,1)}, pred[4,16]{0,1:T(8,128)(4,...) while((s32[]{:T(128)}, f32[512,4,64]{0,2,1:T(8,128)S(1)}, ...), condition=%wide.region_14.15_spmd.clone, body=%wide.region_13.14_spmd.clone.sunk | while | flops 700710912 | bytes 25821680 | solution.py:101
  247.3 4.5 fusion.136
  252.5 3.2 fusion.138
  261.5 4.5 fusion.136
  266.7 3.2 fusion.138
  275.7 4.5 fusion.136
  280.9 3.2 fusion.138
  289.9 4.5 fusion.136
  295.1 3.2 fusion.138
  299.8 4.0 copy.51
  305.9 57.8 %reduce-scatter.4.cloned.1.call-done = bf16[128,512]{1,0:T(8,128)(2,1)} async-done(((bf16[2048,512]{1,0:T(8,128)(2,1)}), bf16[128,512]{1,0:T(8,128)(2,1)}) %reduce-scatter.4.cloned.1.call-update) | async-done | bytes 131088
  363.7 1.8 convolution_bitcast_fusion.3
  365.5 1.8 convolution_bitcast_fusion.4
  370.2 1.7 fusion.35
  371.9 258.1 %all-reduce.3.cloned.1.call-done = (f32[256,256]{0,1:T(8,128)}, f32[256,256]{0,1:T(8,128)}, f32[256,256]{0,1:T(8,128)}, f32[256,256]{1,0:T(8,128)}) async-done(((f32[256,256]{0,1:T(8,128)}, f32[256,256]{0,1:T(8,128)}, f32[256,256]{0,1:T(8,128)}, f32[256,256]{1,0:T(8,128)}), (f32[256,256]{0,1:T(8,128)}, f32[256,256]{0,1:T(8,128)}, f32[256,256]{0,1:T(8,128)}, ...) | async-done | bytes 1048592 | tf_op jit(solution)/shard_map/psum | solution.py:246
  630.0 1.8 copy.44
  631.8 1.8 copy.45
  633.6 1.8 copy.46
  635.4 1.7 copy.123
  (151 shorter events, 70.5 us)
Async XLA Ops:
  7.2 4.5 copy-start
  7.2 46.9 %all-gather.6.cloned.1.call-start = ((), (), s32[]{:S(2)}) async-start(), calls=%async_computation.1 | async-start | bytes 2228224 | tf_op jit(solution)/shard_map/all_gather | solution.py:56
  10.2 353.6 %reduce-scatter.4.cloned.1.call-start = ((), (), s32[]{:S(2)}) async-start(), calls=%async_computation.2 | async-start | bytes 2228224
  299.8 4.2 copy-start.1
  299.8 4.2 copy-start.3
  299.8 5.2 copy-start.2
  299.8 63.9 %copy-start.4 = (bf16[1,128,256]{2,1,0:T(8,128)(2,1)S(1)}, bf16[1,128,256]{2,1,0:T(8,128)(2,1)}, u32[]{:S(2)}) copy-start(bf16[1,128,256]{2,1,0:T(8,128)(2,1)} %param.17) | copy-start | bytes 196612
  303.8 64.4 %copy-start.5 = (bf16[256,256]{1,0:T(8,128)(2,1)S(1)}, bf16[256,256]{1,0:T(8,128)(2,1)}, u32[]{:S(2)}) copy-start(bf16[256,256]{1,0:T(8,128)(2,1)} %param.22) | copy-start | bytes 393220
  303.8 65.4 %copy-start.7 = (bf16[256,256]{1,0:T(8,128)(2,1)S(1)}, bf16[256,256]{1,0:T(8,128)(2,1)}, u32[]{:S(2)}) copy-start(bf16[256,256]{1,0:T(8,128)(2,1)} %param.20) | copy-start | bytes 393220
  303.8 66.4 %copy-start.6 = (bf16[256,256]{1,0:T(8,128)(2,1)S(1)}, bf16[256,256]{1,0:T(8,128)(2,1)}, u32[]{:S(2)}) copy-start(bf16[256,256]{1,0:T(8,128)(2,1)} %param.21) | copy-start | bytes 393220
  303.8 326.2 %all-reduce.3.cloned.1.call-start = ((), (), s32[]{:S(2)}) async-start(), calls=%async_computation.3 | async-start | bytes 2097152 | tf_op jit(solution)/shard_map/psum | solution.py:246
Sparse Core Ops, SparseCore 0:
  10.4 43.6 all-gather.5
  304.0 59.7 reduce-scatter.3
  370.1 259.8 all-reduce.2
where the time goes:
time: 648 us; the launch traced here: 644 us
  waiting for transfers between devices  355 us (55%)
  matrix products  91.2 us (14%)
  blocking collectives  77.3 us (12%)
  local copies, waits for them, and re-layouts  58.9 us (9%)
  other arithmetic  46.1 us (7%)
  between operations  13.9 us (2%)
    psum x1, waiting for transfers between devices, on_device(): lax.psum((weight_query, weight_key, weight_value, weight_out), ('scan', '...  258 us
    unnamed x4, waiting for transfers between devices  57.9 us
    psum x1, blocking collectives, on_device(): col_dot = lax.psum(col_dot, 'blk')  44 us
    all_gather x1, waiting for transfers between devices, on_device(): lax.all_gather(jnp.concatenate([key_local, value_local], axis=1), 'blk',...  39.3 us
    all_gather x2, blocking collectives, combined_all(): gathered = jax.tree.map(lambda a: lax.all_gather(a, axis), part)  33.2 us
    dot_general x12, matrix products, raw_scores(): jnp.einsum('ihc,jhc->hij', query_heads, key_heads(first_row, tile_rows),...  24.4 us
    add x15, other arithmetic, combine_stats(): first_stats[1] * jnp.exp(first_stats[0] - peak_now)  21.3 us
    dot_general x4, matrix products, score_grads(): jnp.einsum('ihc,jhc->hij', grad_heads, value_heads(first_row, tile_rows),...  17.8 us
  transfers between devices with their start and end apart: 3, of which 3 were waited for; matrix products, arithmetic and copies ran while one was open for 2% of the time, Pallas kernels for 0%

commit v1 on v0

v1 whole, which is shorter than its diff:
```python
import functools
import math

import jax
import jax.numpy as jnp
from jax import lax
from jax.experimental import pallas as pl
from jax.experimental.pallas import tpu as pltpu
from jax.sharding import PartitionSpec as P

HEADS = 4
HEAD_DIM = 64
BLOCK = 128
D = 256
ROWS = 512
KEYS = 2048
TILE = 256
TILES = KEYS // TILE
QBLOCKS = ROWS // BLOCK
CHIPS = 8
PLANE = 16
NEG = -1.0e30
LOG2E = math.log2(math.e)
SCALE = HEAD_DIM**-0.5
F32 = jnp.float32
BF16 = jnp.bfloat16
MESH = pl.DeviceIdType.MESH
VMEM = pl.BlockSpec(memory_space=pltpu.VMEM)
SMEM = pl.BlockSpec(memory_space=pltpu.SMEM)


def nn(a, b):
    return jnp.dot(a, b, preferred_element_type=F32)


def nt(a, b):
    return lax.dot_general(a, b, (((1,), (1,)), ((), ())), preferred_element_type=F32)


def lane_mask(rows, parity):
    lane = lax.broadcasted_iota(jnp.int32, (rows, BLOCK), 1)
    return (lane < HEAD_DIM) if parity == 0 else (lane >= HEAD_DIM)


def one_head(array, head, rows):
    group = head // 2
    part = array[:, group * BLOCK : (group + 1) * BLOCK]
    return jnp.where(lane_mask(rows, head % 2), part, jnp.zeros_like(part))


def group_cols(head):
    return slice((head // 2) * BLOCK, (head // 2 + 1) * BLOCK)


def tile_rows(tile):
    return pl.ds(pl.multiple_of(tile * TILE, TILE), TILE)


def block_bias(inter, qb, kb):
    return jnp.where(inter[qb, kb] == 1, 0.0, NEG).astype(F32)


def scaled_tile(scores, inter, tile):
    out = []
    for qb in range(QBLOCKS):
        row = []
        for kb in range(TILE // BLOCK):
            piece = scores[qb * BLOCK : (qb + 1) * BLOCK, kb * BLOCK : (kb + 1) * BLOCK]
            row.append(piece * (SCALE * LOG2E) + block_bias(inter, qb, tile * (TILE // BLOCK) + kb))
        out.append(row)
    return out


def stats_kernel(ref, src, wq, wk, inter, q_out, k_out, lr_out, lc_out, t_scr, rm_scr):
    q_out[...] = nn(ref[...], wq[...]).astype(BF16)

    @pl.loop(0, TILES)
    def _(tile):
        k_out[tile_rows(tile), :] = nn(src[tile_rows(tile), :], wk[...]).astype(BF16)

    for head in range(HEADS):
        qm = one_head(q_out[...], head, ROWS)
        cols = group_cols(head)
        rm_scr[...] = jnp.full_like(rm_scr, -3.0e38)

        @pl.loop(0, TILES)
        def _(tile):
            scores = nt(qm, k_out[tile_rows(tile), cols])
            pieces = scaled_tile(scores, inter, tile)
            for qb in range(QBLOCKS):
                rows = slice(qb * BLOCK, (qb + 1) * BLOCK)
                rm_scr[rows, :] = jnp.maximum(rm_scr[rows, :], jnp.maximum(pieces[qb][0], pieces[qb][1]))
                for kb in range(2):
                    t_scr[tile, rows, kb * BLOCK : (kb + 1) * BLOCK] = pieces[qb][kb]
            for kb in range(2):
                peak = pieces[0][kb]
                for qb in range(1, QBLOCKS):
                    peak = jnp.maximum(peak, pieces[qb][kb])
                peak = peak.max(axis=0, keepdims=True)
                total = jnp.exp2(pieces[0][kb] - peak)
                for qb in range(1, QBLOCKS):
                    total = total + jnp.exp2(pieces[qb][kb] - peak)
                total = total.sum(axis=0, keepdims=True)
                lc_out[pl.ds(head * 16 + tile * 2 + kb, 1), :] = peak + jnp.log2(total)

        peak = rm_scr[...].max(axis=1, keepdims=True)
        rm_scr[...] = jnp.zeros_like(rm_scr)

        @pl.loop(0, TILES)
        def _(tile):
            rm_scr[...] += jnp.exp2(t_scr[tile, :, :BLOCK] - peak) + jnp.exp2(t_scr[tile, :, BLOCK:] - peak)

        total = rm_scr[...].sum(axis=1, keepdims=True)
        lr_out[head] = jnp.broadcast_to(peak + jnp.log2(total), (ROWS, BLOCK))


def probs(qm, k_ref, inter, lr, lc, head, tile):
    pieces = scaled_tile(nt(qm, k_ref[tile_rows(tile), group_cols(head)]), inter, tile)
    row, col = [], []
    for qb in range(QBLOCKS):
        lr_piece = lr[head, qb * BLOCK : (qb + 1) * BLOCK, :]
        row.append([jnp.exp2(pieces[qb][kb] - lr_piece) for kb in range(2)])
        col.append([
            jnp.exp2(pieces[qb][kb] - lc[pl.ds(head * 16 + tile * 2 + kb, 1), :]) for kb in range(2)
        ])
    return row, col


def joined(grid):
    return jnp.concatenate([jnp.concatenate(row, axis=1) for row in grid], axis=0)


def pack_weight(w_out, core, which, matrix):
    for half in range(2):
        for part in range(4):
            w_out[core, 4 * (2 * which + half) + part] = matrix[
                64 * part : 64 * (part + 1), half * BLOCK : (half + 1) * BLOCK
            ].astype(BF16)


def forward_kernel(
    ref, gout, src, q, k, wv, wo, inter, lr, lc,
    v_out, ga_out, gvt_out, cd_out, rd_out, matched_out, w_out,
    vt_scr, gat_scr, att_scr, att_all, gvt_scr, p_scr,
):
    ga_out[...] = nt(gout[...], wo[...]).astype(BF16)
    gat_scr[...] = nt(wo[...], gout[...]).astype(BF16)
    wvt = wv[...].T

    @pl.loop(0, TILES)
    def _(tile):
        rows = src[tile_rows(tile), :]
        v_out[tile_rows(tile), :] = nn(rows, wv[...]).astype(BF16)
        vt_scr[tile] = nt(wvt, rows).astype(BF16)

    for head in range(HEADS):
        qm = one_head(q[...], head, ROWS)
        cols = group_cols(head)
        lanes = slice(head * HEAD_DIM, (head + 1) * HEAD_DIM)
        gat = gat_scr[lanes, :]
        att_scr[...] = jnp.zeros_like(att_scr)

        @pl.loop(0, TILES)
        def _(tile):
            row, col = probs(qm, k, inter, lr, lc, head, tile)
            match = joined([[(row[a][b] * col[a][b]).astype(BF16) for b in range(2)] for a in range(QBLOCKS)])
            att_scr[...] += nn(match, v_out[tile_rows(tile), cols])
            gvt = nn(gat, match)
            gvt_scr[tile, lanes, :] = gvt.astype(BF16)
            dots = (gvt * vt_scr[tile, lanes, :].astype(F32)).sum(axis=0, keepdims=True)
            for kb in range(2):
                cd_out[pl.ds(head * 16 + tile * 2 + kb, 1), :] = dots[:, kb * BLOCK : (kb + 1) * BLOCK]

        mask = lane_mask(ROWS, head % 2)
        att = jnp.where(mask, att_scr[...], 0.0)
        rd = (att * ga_out[:, cols].astype(F32)).sum(axis=1, keepdims=True)
        rd_out[head] = jnp.broadcast_to(rd, (ROWS, BLOCK))
        if head % 2 == 0:
            att_all[:, cols] = att.astype(BF16)
        else:
            att_all[:, cols] = jnp.where(mask, att.astype(BF16), att_all[:, cols])

    matched_out[...] = (ref[...].astype(F32) + nn(att_all[...], wo[...])).astype(BF16)
    gvt_out[...] = gvt_scr[...]
    pack_weight(w_out, 0, 1, nn(att_all[...].T, gout[...]))
    wvg = jnp.zeros((D, D), F32)
    for tile in range(TILES):
        wvg = wvg + nn(gvt_scr[tile], src[tile * TILE : (tile + 1) * TILE, :])
    pack_weight(w_out, 0, 0, wvg.T)


def backward_kernel(
    ref, gout, src, q, k, v, ga, wq, wk, wv, inter, lr, lc, rd, cd, gvt, w_in,
    gref_out, gs_out, w_out,
    gkt_scr, gq_scr, gq_all,
):
    qt = q[...].T
    for head in range(HEADS):
        qm = one_head(q[...], head, ROWS)
        gam = one_head(ga[...], head, ROWS)
        cols = group_cols(head)
        lanes = slice(head * HEAD_DIM, (head + 1) * HEAD_DIM)
        qt_head = qt[lanes, :]
        gq_scr[...] = jnp.zeros_like(gq_scr)

        @pl.loop(0, TILES)
        def _(tile):
            row, col = probs(qm, k, inter, lr, lc, head, tile)
            gp = nt(gam, v[tile_rows(tile), cols])
            grid = []
            for qb in range(QBLOCKS):
                rows = slice(qb * BLOCK, (qb + 1) * BLOCK)
                rd_piece = rd[head, rows, :]
                line = []
                for kb in range(2):
                    cd_piece = cd[pl.ds(head * 16 + tile * 2 + kb, 1), :]
                    r, c = row[qb][kb], col[qb][kb]
                    match = (r * c).astype(BF16).astype(F32)
                    g = gp[rows, kb * BLOCK : (kb + 1) * BLOCK]
                    line.append((2.0 * match * g - r * rd_piece - c * cd_piece).astype(BF16))
                grid.append(line)
            gs = joined(grid)
            gq_scr[...] += nn(gs, k[tile_rows(tile), cols])
            gkt_scr[tile, lanes, :] = (nn(qt_head, gs) * SCALE).astype(BF16)

        mask = lane_mask(ROWS, head % 2)
        gq = (gq_scr[...] * SCALE).astype(BF16)
        if head % 2 == 0:
            gq_all[:, cols] = gq
        else:
            gq_all[:, cols] = jnp.where(mask, gq, gq_all[:, cols])

    gref_out[...] = (gout[...].astype(F32) + nt(gq_all[...], wq[...])).astype(BF16)
    pack_weight(w_out, 0, 0, nn(ref[...].T, gq_all[...]))
    wkg = jnp.zeros((D, D), F32)
    for tile in range(TILES):
        wkg = wkg + nn(gkt_scr[tile], src[tile * TILE : (tile + 1) * TILE, :])
        gst = nn(wk[...], gkt_scr[tile]) + nn(wv[...], gvt[tile])
        gs_out[0, tile] = gst[:, :BLOCK].astype(BF16)
        gs_out[1, tile] = gst[:, BLOCK:].astype(BF16)
    pack_weight(w_out, 0, 1, wkg.T)
    w_out[1] = w_in[0]


def place():
    blk = lax.axis_index("blk")
    scan = lax.axis_index("scan")
    chip = lax.div(blk, 2)
    core = lax.rem(blk, 2)
    return scan, blk, chip, core


def on_column(chip, core):
    return {"blk": chip * 2 + core}


def meet(targets):
    barrier = pltpu.get_barrier_semaphore()
    for target in targets:
        pl.semaphore_signal(barrier, inc=1, device_id=target, device_id_type=MESH)
    pl.semaphore_wait(barrier, len(targets))


def send(src, dst, sems, index, target):
    send_sem, recv_sem = sems
    return pltpu.make_async_remote_copy(
        src_ref=src, dst_ref=dst, send_sem=send_sem.at[index], recv_sem=recv_sem.at[index],
        device_id=target, device_id_type=MESH,
    )


FAR_FIRST = (4, 3, 5, 2, 6, 1, 7)


def gather_kernel(src, out, own_sem, s0, r0, s1, r1):
    scan, blk, chip, core = place()
    partner = {"blk": chip * 2 + 1 - core}
    peers = [on_column(lax.rem(chip + d, CHIPS), core) for d in range(1, CHIPS)]
    meet([partner] + peers)
    across = {}
    for d in FAR_FIRST:
        across[d] = send(src, out.at[blk], (s0, r0), d, peers[d - 1])
        across[d].start()
    forward = [send(src, out.at[blk], (s1, r1), 0, partner)]
    forward[0].start()
    own = pltpu.make_async_copy(src, out.at[blk], own_sem)
    own.start()
    for d in (1, 7, 2, 6, 3, 5, 4):
        across[d].wait_recv()
        origin = lax.rem(chip + CHIPS - d, CHIPS) * 2 + core
        copy = send(out.at[origin], out.at[origin], (s1, r1), d, partner)
        copy.start()
        forward.append(copy)
    own.wait()
    for copy in forward:
        copy.wait_recv()
    for copy in forward:
        copy.wait_send()
    for copy in across.values():
        copy.wait_send()


def exchange_kernel(combine, part, out, buf_a, half, buf_b, done, s0, r0, s1, r1):
    scan, blk, chip, core = place()
    partner = {"blk": chip * 2 + 1 - core}
    peers = [on_column(lax.rem(chip + d, CHIPS), core) for d in range(1, CHIPS)]
    meet([partner] + peers)
    mine = pl.ds(pl.multiple_of(core * 32, 32), 32)
    other = pl.ds(pl.multiple_of((1 - core) * 32, 32), 32)
    first = send(part.at[other], buf_a, (s0, r0), 0, partner)
    first.start()
    first.wait_recv()
    half[...] = combine([part[mine], buf_a[...]])
    across = {}
    for d in FAR_FIRST:
        across[d] = send(half, buf_b.at[d - 1], (s1, r1), d - 1, peers[d - 1])
        across[d].start()
    for d in (1, 7, 2, 6, 3, 5, 4):
        across[d].wait_recv()
    done[...] = combine([half[...]] + [buf_b[d] for d in range(CHIPS - 1)])
    last = send(done, out.at[mine], (s0, r0), 1, partner)
    last.start()
    out[mine] = done[...]
    last.wait_recv()
    first.wait_send()
    for copy in across.values():
        copy.wait_send()
    last.wait_send()


def log_sum(parts):
    peak = functools.reduce(jnp.maximum, parts)
    return peak + jnp.log2(sum(jnp.exp2(part - peak) for part in parts))


def plain_sum(parts):
    return sum(parts)


def final_kernel(
    gs, wg, gsrc_out, wq_out, wk_out, wv_out, wo_out,
    wbuf, gbuf, wsum, gsum, wrecv, grecv, wpart, zrecv, wdone, zall, wrow, wall,
    sp, rp, sx, rx, sg, rg, sz, rz, sa, ra, sb, rb,
):
    scan, blk, chip, core = place()
    partner = {"blk": chip * 2 + 1 - core}
    peers = [on_column(lax.rem(chip + d, CHIPS), core) for d in range(1, CHIPS)]
    plane = [{"scan": lax.rem(scan + d, PLANE)} for d in range(1, PLANE)]
    meet([partner] + peers + plane)
    copies = []

    def start(*args):
        copy = send(*args)
        copy.start()
        copies.append(copy)
        return copy

    w_swap = start(wg.at[1 - core], wbuf, (sp, rp), 0, partner)
    g_swap = start(gs.at[1 - core], gbuf, (sp, rp), 1, partner)
    w_swap.wait_recv()
    wsum[...] = (wg[core].astype(F32) + wbuf[...].astype(F32)).astype(BF16)
    plane_in = []
    for d in range(1, PLANE):
        to = lax.rem(scan + d, PLANE)
        plane_in.append(start(wsum.at[to], wrecv.at[d - 1], (sx, rx), d - 1, plane[d - 1]))
    g_swap.wait_recv()
    for c in range(CHIPS):
        gsum[c] = (gs[core, c].astype(F32) + gbuf[c].astype(F32)).astype(BF16)
    col_in = []
    for d in FAR_FIRST:
        to = lax.rem(chip + d, CHIPS)
        col_in.append(start(gsum.at[to], grecv.at[d - 1], (sg, rg), d - 1, peers[d - 1]))
    for copy in plane_in:
        copy.wait_recv()
    total = wsum[scan].astype(F32)
    for d in range(PLANE - 1):
        total = total + wrecv[d].astype(F32)
    wpart[...] = total.reshape(CHIPS, 8, BLOCK)
    z_in = []
    for d in range(1, CHIPS):
        to = lax.rem(chip + d, CHIPS)
        z_in.append(start(wpart.at[to], zrecv.at[d - 1], (sz, rz), d - 1, peers[d - 1]))
    for copy in z_in:
        copy.wait_recv()
    total = wpart[chip]
    for d in range(CHIPS - 1):
        total = total + zrecv[d]
    wdone[...] = total
    a_in = []
    for d in range(1, CHIPS):
        a_in.append(start(wdone, zall.at[chip], (sa, ra), d - 1, peers[d - 1]))
    zall[chip] = total
    for copy in col_in:
        copy.wait_recv()
    gsrc = gsum[chip].astype(F32)
    for d in range(CHIPS - 1):
        gsrc = gsrc + grecv[d].astype(F32)
    gsrc_out[...] = gsrc.T.astype(BF16)
    for copy in a_in:
        copy.wait_recv()
    row = zall[...].reshape(CHIPS * 8, BLOCK).astype(BF16)
    wrow[...] = row
    b_in = []
    for d in range(1, PLANE):
        b_in.append(start(wrow, wall.at[core, scan], (sb, rb), d - 1, plane[d - 1]))
    wall[core, scan] = row
    for copy in b_in:
        copy.wait_recv()
    last = start(wall.at[core], wall.at[core], (sp, rp), 2, partner)
    last.wait_recv()
    for core_at, pair in enumerate(((wq_out, wk_out), (wv_out, wo_out))):
        for which, out in enumerate(pair):
            for half in range(2):
                for part in range(4):
                    out[64 * part : 64 * (part + 1), half * BLOCK : (half + 1) * BLOCK] = wall[
                        core_at, 4 * (2 * which + half) + part
                    ].astype(F32)
    for copy in copies:
        copy.wait_send()


def shape(dims, dtype):
    return jax.ShapeDtypeStruct(dims, dtype)


DMA = pltpu.SemaphoreType.DMA


def call(kernel, outs, n_in, scratch, name, smem=(), collective_id=None, vmem=48 << 20):
    params = dict(vmem_limit_bytes=vmem)
    if collective_id is not None:
        params.update(collective_id=collective_id, has_side_effects=True)
    single = not isinstance(outs, (list, tuple))
    return pl.pallas_call(
        kernel,
        out_shape=outs,
        in_specs=[SMEM if i in smem else VMEM for i in range(n_in)],
        out_specs=VMEM if single else [VMEM] * len(outs),
        scratch_shapes=scratch,
        compiler_params=pltpu.CompilerParams(**params),
        name=name,
    )


def gather(src):
    out = call(
        gather_kernel, shape((16, BLOCK, D), BF16), 1,
        [DMA, DMA((8,)), DMA((8,)), DMA((8,)), DMA((8,))], "gather_src", collective_id=1,
    )(src)
    return out.reshape(KEYS, D)


def exchange(part, combine, ident):
    return call(
        functools.partial(exchange_kernel, combine), shape((64, BLOCK), F32), 1,
        [pltpu.VMEM((32, BLOCK), F32), pltpu.VMEM((32, BLOCK), F32), pltpu.VMEM((7, 32, BLOCK), F32),
         pltpu.VMEM((32, BLOCK), F32), DMA((2,)), DMA((2,)), DMA((7,)), DMA((7,))],
        "exchange_%d" % ident, collective_id=ident,
    )(part)


def stats(ref, src, wq, wk, inter):
    return call(
        stats_kernel,
        [shape((ROWS, D), BF16), shape((KEYS, D), BF16), shape((HEADS, ROWS, BLOCK), F32), shape((64, BLOCK), F32)],
        5, [pltpu.VMEM((TILES, ROWS, TILE), F32), pltpu.VMEM((ROWS, BLOCK), F32)], "stats", smem=(4,),
    )(ref, src, wq, wk, inter)


def forward(ref, gout, src, q, k, wv, wo, inter, lr, lc):
    return call(
        forward_kernel,
        [shape((KEYS, D), BF16), shape((ROWS, D), BF16), shape((TILES, D, TILE), BF16), shape((64, BLOCK), F32),
         shape((HEADS, ROWS, BLOCK), F32), shape((ROWS, D), BF16), shape((1, 16, 64, BLOCK), BF16)],
        10,
        [pltpu.VMEM((TILES, D, TILE), BF16), pltpu.VMEM((D, ROWS), BF16), pltpu.VMEM((ROWS, BLOCK), F32),
         pltpu.VMEM((ROWS, D), BF16), pltpu.VMEM((TILES, D, TILE), BF16), pltpu.VMEM((ROWS, TILE), BF16)],
        "forward", smem=(7,),
    )(ref, gout, src, q, k, wv, wo, inter, lr, lc)


def backward(*args):
    return call(
        backward_kernel,
        [shape((ROWS, D), BF16), shape((2, TILES, D, BLOCK), BF16), shape((2, 16, 64, BLOCK), BF16)],
        17,
        [pltpu.VMEM((TILES, D, TILE), BF16), pltpu.VMEM((ROWS, BLOCK), F32), pltpu.VMEM((ROWS, D), BF16)],
        "backward", smem=(10,),
    )(*args)


def final(gs, wg):
    row = (64, BLOCK)
    return call(
        final_kernel, [shape((BLOCK, D), BF16)] + [shape((D, D), F32)] * 4, 2,
        [pltpu.VMEM((16,) + row, BF16), pltpu.VMEM((8, D, BLOCK), BF16), pltpu.VMEM((16,) + row, BF16),
         pltpu.VMEM((8, D, BLOCK), BF16), pltpu.VMEM((15,) + row, BF16), pltpu.VMEM((7, D, BLOCK), BF16),
         pltpu.VMEM((8, 8, BLOCK), F32), pltpu.VMEM((7, 8, BLOCK), F32), pltpu.VMEM((8, BLOCK), F32),
         pltpu.VMEM((8, 8, BLOCK), F32), pltpu.VMEM(row, BF16), pltpu.VMEM((2, 16) + row, BF16)]
        + [DMA((n,)) for n in (3, 3, 15, 15, 7, 7, 7, 7, 7, 7, 15, 15)],
        "final", collective_id=4,
    )(gs, wg)


def on_device(ref_feats, src_feats, grad_out, w_query, w_key, w_value, w_out, intersection):
    ref, gout, inter = ref_feats[0], grad_out[0], intersection[0]
    src = gather(src_feats[0])
    q, k, lr, lc = stats(ref, src, w_query, w_key, inter)
    lc = exchange(lc, log_sum, 2)
    v, ga, gvt, cd, rd, matched, w_part = forward(ref, gout, src, q, k, w_value, w_out, inter, lr, lc)
    cd = exchange(cd, plain_sum, 3)
    gref, gs, wg = backward(
        ref, gout, src, q, k, v, ga, w_query, w_key, w_value, inter, lr, lc, rd, cd, gvt, w_part
    )
    gsrc, wqg, wkg, wvg, wog = final(gs, wg)
    return matched[None], gref[None], gsrc[None], wqg, wkg, wvg, wog


def solution(mesh):
    split = P("scan", "blk", None)
    return jax.shard_map(
        on_device, mesh=mesh,
        in_specs=(split, split, split, P(), P(), P(), P(), split),
        out_specs=(split, split, split, P(), P(), P(), P()),
        check_vma=False,
    )
```

time: 648 us -> 150 us (0.23)
  waiting for transfers between devices: 355 us -> 0 us
  Pallas kernels: 0 us -> 140 us
  matrix products: 91.2 us -> 0 us
  blocking collectives: 77.3 us -> 0 us
  local copies, waits for them, and re-layouts: 58.9 us -> 9.24 us
  other arithmetic: 46.1 us -> 0 us
  between operations: 13.9 us -> 0.8 us
    psum x1 -> x0, waiting for transfers between devices: 258 us -> none  [on_device(): lax.psum((weight_query, weight_key, weight_value, weight_out), ('scan', '...]
    pallas_call x0 -> x7, Pallas kernels: none -> 140 us  [the longest x1 36 us: final(): call(final_kernel, [shape((BLOCK, D), BF16)] + [shape((D, D), F32)] * 4,...]
    dot_general x48 -> x0, matrix products: 91.2 us -> none  [the longest x12 24.4 us: raw_scores(): jnp.einsum('ihc,jhc->hij', query_heads, key_heads(first_row, tile_rows),...]
    unnamed x4 -> x0, waiting for transfers between devices: 57.9 us -> none
    psum x1 -> x0, blocking collectives: 44 us -> none  [on_device(): col_dot = lax.psum(col_dot, 'blk')]
    all_gather x1 -> x0, waiting for transfers between devices: 39.3 us -> none  [on_device(): lax.all_gather(jnp.concatenate([key_local, value_local], axis=1), 'blk',...]
    dynamic_slice x46 -> x0, local copies, waits for them, and re-layouts: 36.8 us -> none  [the longest x12 8.3 us: mask_blocks(): lax.dynamic_slice_in_dim(blocks, first_row // BLOCK, tile_rows // BLOCK, 1)]
    all_gather x2 -> x0, blocking collectives: 33.2 us -> none  [combined_all(): gathered = jax.tree.map(lambda a: lax.all_gather(a, axis), part)]
  transfers between devices with their start and end apart: 3 -> 0, of which waited for: 3 -> 0; matrix products, arithmetic and copies ran while one was open for 2% -> 0% of each run, Pallas kernels for 0% -> 0%
where the time goes in v1:
time: 150 us
  Pallas kernels  140 us (93%)
  local copies, waits for them, and re-layouts  9.24 us (6%)
    pallas_call x1, Pallas kernels, final(): call(final_kernel, [shape((BLOCK, D), BF16)] + [shape((D, D), F32)] * 4,...  36 us
    pallas_call x1, Pallas kernels, gather(): call(gather_kernel, shape((16, BLOCK, D), BF16), 1, [DMA, DMA((8,)), DMA(...  23.1 us
    pallas_call x1, Pallas kernels, backward(): call(backward_kernel, [shape((ROWS, D), BF16), shape((2, TILES, D, BLOCK)...  22.5 us
    pallas_call x2, Pallas kernels, exchange(): call(functools.partial(exchange_kernel, combine), shape((64, BLOCK), F32)...  21.7 us
    pallas_call x1, Pallas kernels, forward(): call(forward_kernel, [shape((KEYS, D), BF16), shape((ROWS, D), BF16), sha...  19.9 us
    pallas_call x1, Pallas kernels, stats(): call(stats_kernel, [shape((ROWS, D), BF16), shape((KEYS, D), BF16), shape...  16.8 us
    unnamed x33, local copies, waits for them, and re-layouts  9.24 us

profile of v1, /device:TPU:1, one launch (start us, length us, event | category | flops | bytes accessed | tf_op | source)
XLA Modules:
  0.0 150.0 jit_solution(12062071484677850225)
XLA Ops:
  0.6 0.0 copy-start.12
  0.6 0.8 copy-done.12
  1.5 0.0 copy-start.3
  1.5 0.0 copy-start.8
  1.5 0.0 copy-start.9
  1.5 0.0 copy-start.13
  1.5 23.1 %gather_src.1 = bf16[16,128,256]{2,1,0:T(8,128)(2,1)S(1)} custom-call(bf16[128,256]{1,0:T(8,128)(2,1)S(1)} %bitcast.16), custom_call_target="tpu_custom_call" | custom-call | tf_op jit(solution)/shard_map/gather_src/pallas_call | solution.py:446
  24.6 0.0 copy-done.3
  24.6 0.0 copy-done.8
  24.6 0.0 copy-done.9
  24.6 0.0 copy-done.13
  24.6 0.0 copy-start.7
  24.7 0.0 copy-start.10
  24.7 0.0 copy-start.11
  24.7 16.8 %stats.1 = (bf16[512,256]{1,0:T(8,128)(2,1)S(1)}, bf16[2048,256]{1,0:T(8,128)(2,1)S(1)}, f32[4,512,128]{2,1,0:T(8,128)S(1)}, f32[64,128]{1,0:T(8,128)S(1)}) custom-call(bf16[512,256]{1,0:T(8,128)(2,1)S(1)} %bitcast.11, bf16[2048,256]{1,0:T(8,128)(2,1)S(1)} %bitcast.8, bf16[256,256]{1,0:T(8,128)(2,1)S(1)} %copy-done.8, bf16[256,256]{1,0:T(8,128)(2,1)S(1)} %copy-done.9, ...), custom_call_target="tpu_custom_call" | custom-call | tf_op jit(solution)/shard_map/stats/pallas_call | solution.py:463
  41.5 0.0 copy-start
  41.5 1.0 copy-done
  42.5 0.0 copy-start.2
  42.5 1.0 copy-done.2
  43.5 10.8 %exchange_2.1.lc = f32[64,128]{1,0:T(8,128)S(1)} custom-call(f32[64,128]{1,0:T(8,128)S(1)} %get-tuple-element.29.part), custom_call_target="tpu_custom_call" | custom-call | tf_op jit(solution)/shard_map/exchange_2/pallas_call | solution.py:454
  54.3 0.0 copy-done.7
  54.3 0.0 copy-done.10
  54.3 0.0 copy-done.11
  54.3 0.0 copy-start.1
  54.3 19.9 %forward.1 = (bf16[2048,256]{1,0:T(8,128)(2,1)S(1)}, bf16[512,256]{1,0:T(8,128)(2,1)S(1)}, bf16[8,256,256]{2,1,0:T(8,128)(2,1)S(1)}, f32[64,128]{1,0:T(8,128)S(1...) custom-call(bf16[512,256]{1,0:T(8,128)(2,1)S(1)} %bitcast.12, ...), custom_call_target="tpu_custom_call" | custom-call | tf_op jit(solution)/shard_map/forward/pallas_call | solution.py:471
  74.2 0.0 copy-start.4
  74.2 1.0 copy-done.4
  75.2 0.0 copy-start.5
  75.2 1.0 copy-done.5
  76.2 0.0 copy-start.6
  76.2 1.0 copy-done.6
  77.2 11.0 %exchange_3.1.cd = f32[64,128]{1,0:T(8,128)S(1)} custom-call(f32[64,128]{1,0:T(8,128)S(1)} %get-tuple-element.34.part), custom_call_target="tpu_custom_call" | custom-call | tf_op jit(solution)/shard_map/exchange_3/pallas_call | solution.py:454
  88.1 0.0 copy-done.1
  88.1 22.5 %backward.1 = (bf16[512,256]{1,0:T(8,128)(2,1)}, bf16[2,8,256,128]{3,2,1,0:T(8,128)(2,1)S(1)}, bf16[2,16,64,128]{3,2,1,0:T(8,128)(2,1)S(1)}) custom-call(bf16[512,256]{1,0:T(8,128)(2,1)S(1)} %bitcast.13, bf16[512,256]{1,0:T(8,128)(2,1)S(1)} %bitcast.15, bf16[2048,256]{1,0:T(8,128)(2,1)S(1)} %bitcast.10, bf16[512,256]{1,0:T(8,128)(2,1)S(1)} %get-tuple-element.26.q, ...), custom_call_target="tpu_custom_call" | custom-call | tf_op jit(solution)/shard_map/backward/pallas_call | solution.py:483
  110.6 36.0 %final.1 = (bf16[128,256]{1,0:T(8,128)(2,1)S(1)}, f32[256,256]{1,0:T(8,128)S(1)}, f32[256,256]{1,0:T(8,128)S(1)}, f32[256,256]{1,0:T(8,128)S(1)}, f32[256,256]{1,0:T(8,128)S(1)}) custom-call(bf16[2,8,256,128]{3,2,1,0:T(8,128)(2,1)S(1)} %get-tuple-element.38.gs, bf16[2,16,64,128]{3,2,1,0:T(8,128)(2,1)S(1)} %get-tuple-element.39.wg), custom_call_target="tpu_custom_call" | custom-call | tf_op jit(solution)/shard_map/final/pallas_call | solution.py:494
  146.6 0.6 copy.20
  147.2 0.7 copy.21
  147.9 0.7 copy.22
  148.6 0.7 copy.23
  149.3 0.7 copy.24
Async XLA Ops:
  0.6 0.8 copy-start.12
  1.5 23.1 %copy-start.3 = (bf16[1,512,256]{2,1,0:T(8,128)(2,1)S(1)}, bf16[1,512,256]{2,1,0:T(8,128)(2,1)}, u32[]{:S(2)}) copy-start(bf16[1,512,256]{2,1,0:T(8,128)(2,1)} %param.8) | copy-start | bytes 786436
  1.5 23.1 %copy-start.8 = (bf16[256,256]{1,0:T(8,128)(2,1)S(1)}, bf16[256,256]{1,0:T(8,128)(2,1)}, u32[]{:S(2)}) copy-start(bf16[256,256]{1,0:T(8,128)(2,1)} %wq.3) | copy-start | bytes 393220
  1.5 23.1 %copy-start.9 = (bf16[256,256]{1,0:T(8,128)(2,1)S(1)}, bf16[256,256]{1,0:T(8,128)(2,1)}, u32[]{:S(2)}) copy-start(bf16[256,256]{1,0:T(8,128)(2,1)} %wk.3) | copy-start | bytes 393220
  1.5 23.2 %copy-start.13 = (s32[1,4,16]{2,1,0:T(4,128)S(1)}, s32[1,4,16]{2,1,0:T(4,128)}, u32[]{:S(2)}) copy-start(s32[1,4,16]{2,1,0:T(4,128)} %param.15) | copy-start | bytes 772
  24.6 29.6 %copy-start.7 = (bf16[1,512,256]{2,1,0:T(8,128)(2,1)S(1)}, bf16[1,512,256]{2,1,0:T(8,128)(2,1)}, u32[]{:S(2)}) copy-start(bf16[1,512,256]{2,1,0:T(8,128)(2,1)} %param.10) | copy-start | bytes 786436
  24.7 29.6 %copy-start.10 = (bf16[256,256]{1,0:T(8,128)(2,1)S(1)}, bf16[256,256]{1,0:T(8,128)(2,1)}, u32[]{:S(2)}) copy-start(bf16[256,256]{1,0:T(8,128)(2,1)} %wv.3) | copy-start | bytes 393220
  24.7 29.6 %copy-start.11 = (bf16[256,256]{1,0:T(8,128)(2,1)S(1)}, bf16[256,256]{1,0:T(8,128)(2,1)}, u32[]{:S(2)}) copy-start(bf16[256,256]{1,0:T(8,128)(2,1)} %wo.1) | copy-start | bytes 393220
  41.5 1.0 copy-start
  42.5 1.0 copy-start.2
  54.3 33.8 %copy-start.1 = (bf16[2048,256]{1,0:T(8,128)(2,1)S(1)}, bf16[2048,256]{1,0:T(8,128)(2,1)}, u32[]{:S(2)}) copy-start(bf16[2048,256]{1,0:T(8,128)(2,1)} %copy-done) | copy-start | bytes 3145732
  74.2 1.0 copy-start.4
  75.2 1.0 copy-start.5
  76.2 1.0 copy-start.6

commit v2 on v0

v2 whole, which is shorter than its diff:
```python
import functools
import math

import jax
import jax.numpy as jnp
from jax import lax
from jax.experimental import pallas as pl
from jax.experimental.pallas import tpu as pltpu
from jax.sharding import PartitionSpec as P

HEADS = 4
HEAD_DIM = 64
BLOCK = 128
D = 256
ROWS = 512
KEYS = 2048
TILE = 256
TILES = KEYS // TILE
QBLOCKS = ROWS // BLOCK
KBLOCKS = KEYS // BLOCK
CHIPS = 8
PLANE = 16
NEG = -1.0e30
SCALE = HEAD_DIM**-0.5
UNIT = SCALE * math.log2(math.e)
F32 = jnp.float32
BF16 = jnp.bfloat16
MESH = pl.DeviceIdType.MESH
VMEM = pl.BlockSpec(memory_space=pltpu.VMEM)
SMEM = pl.BlockSpec(memory_space=pltpu.SMEM)
DMA = pltpu.SemaphoreType.DMA


def nn(a, b):
    return jnp.dot(a, b, preferred_element_type=F32)


def nt(a, b):
    return lax.dot_general(a, b, (((1,), (1,)), ((), ())), preferred_element_type=F32)


def by_halves(a, b):
    half = a.shape[0] // 2
    return jnp.concatenate([nn(a[:half], b), nn(a[half:], b)], axis=0)


def lanes_of(rows):
    return lax.broadcasted_iota(jnp.int32, (rows, BLOCK), 1)


def own_lanes(rows, head):
    lane = lanes_of(rows)
    return (lane < HEAD_DIM) if head % 2 == 0 else (lane >= HEAD_DIM)


def spare(head):
    return HEAD_DIM if head % 2 == 0 else 0


def group_cols(head):
    return slice((head // 2) * BLOCK, (head // 2 + 1) * BLOCK)


def head_lanes(head):
    return slice(head * HEAD_DIM, (head + 1) * HEAD_DIM)


def query_extra(inter, head, pieces):
    base = spare(head)
    lane = lanes_of(1)
    grid = []
    for qb in range(QBLOCKS):
        row = jnp.zeros((1, BLOCK), F32)
        for kb in range(KBLOCKS):
            bias = jnp.where(inter[qb, kb] == 1, 0.0, NEG).astype(F32)
            row = jnp.where(lane == base + kb, bias, row)
        grid.append(jnp.broadcast_to(row, (BLOCK, BLOCK)))
    extra = jnp.concatenate(grid, axis=0)
    if pieces is not None:
        lane = lanes_of(ROWS)
        for at, piece in enumerate(pieces):
            extra = jnp.where(lane == base + KBLOCKS + at, piece, extra)
    return extra


def key_extra(tile, head):
    base = spare(head)
    lane = lanes_of(TILE)
    row = lax.broadcasted_iota(jnp.int32, (TILE, BLOCK), 0)
    block = tile * 2 + jnp.where(row >= BLOCK, 1, 0)
    hot = (lane - base == block) | ((lane >= base + KBLOCKS) & (lane < base + KBLOCKS + 3))
    return jnp.where(hot, 1.0, 0.0)


def in_three(value):
    first = value.astype(BF16).astype(F32)
    second = (value - first).astype(BF16).astype(F32)
    third = (value - first - second).astype(BF16).astype(F32)
    return first, second, third


def log_sum(parts):
    peak = functools.reduce(jnp.maximum, parts)
    return peak + jnp.log2(sum(jnp.exp2(part - peak) for part in parts))


def plain_sum(parts):
    return sum(parts)


def pack_weight(wg, core, which, matrix):
    for half in range(2):
        for part in range(4):
            wg[core, 4 * (2 * which + half) + part] = matrix[
                64 * part : 64 * (part + 1), half * BLOCK : (half + 1) * BLOCK
            ].astype(BF16)


def send(src, dst, sems, index, target):
    return pltpu.make_async_remote_copy(
        src_ref=src, dst_ref=dst, send_sem=sems[0].at[index], recv_sem=sems[1].at[index],
        device_id=target, device_id_type=MESH,
    )


def layer_kernel(
    ref, gout, src, wq, wk, wv, wo, inter,
    matched_out, gref_out, gsrc_out, wq_out, wk_out, wv_out, wo_out,
    src_all, k_scr, kh, v_scr, vt_scr, qs, qf, qb_scr, gam, gat_scr, qt_all, t_scr, rm, lr,
    lc_part, lc_swap, lc_chip, lc_in, lc_all, cd_part, cd_swap, cd_chip, cd_in, cd_all,
    att, att_all, gvt_scr, rd_scr, wvg, wkg, gq, gq_all,
    gs_part, gs_swap, gs_sum, gs_in, wg, w_swap, w_sum, w_in, w_part, z_in, w_done, z_all, w_row, w_all,
    own_sem, sa0, ra0, sa1, ra1, sl0, rl0, sl1, rl1, sc0, rc0, sc1, rc1, sg0, rg0, sg1, rg1,
    sp, rp, sx, rx, sz, rz, sy, ry, sb, rb,
):
    blk = lax.axis_index("blk")
    scan = lax.axis_index("scan")
    chip = lax.div(blk, 2)
    core = lax.rem(blk, 2)
    partner = {"blk": chip * 2 + 1 - core}

    def on_chip(offset, core_at):
        return {"blk": lax.rem(chip + offset, CHIPS) * 2 + core_at}

    plane = [{"scan": lax.rem(scan + d, PLANE)} for d in range(1, PLANE)]
    column = [on_chip(d, c) for d in range(1, CHIPS) for c in range(2)]
    barrier = pltpu.get_barrier_semaphore()
    everyone = [partner] + column + plane
    for target in everyone:
        pl.semaphore_signal(barrier, inc=1, device_id=target, device_id_type=MESH)

    q_rows = nn(ref[...], wq[...]).astype(BF16)
    for head in range(HEADS):
        part = q_rows[:, group_cols(head)]
        extra = query_extra(inter, head, None).astype(BF16)
        qs[head] = jnp.where(own_lanes(ROWS, head), part, extra)
    qt_all[...] = q_rows.T
    rm[...] = jnp.full_like(rm, -3.0e38)
    own = pltpu.make_async_copy(src, src_all.at[blk], own_sem)
    own.start()

    pl.semaphore_wait(barrier, len(everyone))
    for d in (4, 3, 5, 2, 6, 1, 7):
        send(src, src_all.at[blk], (sa0, ra0), d, on_chip(d, core)).start()
    send(src, src_all.at[blk], (sa1, ra1), 0, partner).start()

    ga_rows = nt(gout[...], wo[...]).astype(BF16)
    gat_scr[...] = nt(wo[...], gout[...]).astype(BF16)
    for head in range(HEADS):
        part = ga_rows[:, group_cols(head)]
        gam[head] = jnp.where(own_lanes(ROWS, head), part, jnp.zeros_like(part))
    wvt = wv[...].T
    own.wait()

    def near_first(step):
        half = lax.div(step + 1, 2)
        return jnp.where(lax.rem(step, 2) == 1, half, lax.rem(CHIPS - half, CHIPS))

    def far_first(step):
        return jnp.where(lax.rem(step, 2) == 0, 4 + lax.div(step, 2), 4 - lax.div(step + 1, 2))

    def from_offset(d):
        return lax.rem(chip + CHIPS - d, CHIPS)

    def to_offset(d):
        return lax.rem(chip + d, CHIPS)

    def swap_columns(tile, part, swap, sems):
        return send(part.at[tile], swap.at[tile], sems, tile, partner)

    def spread_columns(tile, combine, part, swap, chip_sum, inbox, sems_swap, sems):
        swap_columns(tile, part, swap, sems_swap).wait_recv()
        chip_sum[tile] = combine([part[tile], swap[tile]])
        for d in range(1, CHIPS):
            for c in range(2):
                send(chip_sum.at[tile, core], inbox.at[tile, d - 1, core], sems, tile, on_chip(d, c)).start()

    def collect_columns(tile, combine, chip_sum, inbox, total, sems):
        send(inbox.at[tile], inbox.at[tile], sems, tile, partner).wait_recv()
        total[tile] = combine([chip_sum[tile]] + [inbox[tile, d] for d in range(CHIPS - 1)])

    @pl.loop(0, TILES)
    def _(step):
        d = near_first(step)
        tile = from_offset(d)

        @pl.when(step < TILES - 1)
        def _():
            d_next = near_first(step + 1)
            origin = from_offset(d_next) * 2 + core
            send(src, src_all.at[origin], (sa0, ra0), d_next, partner).wait_recv()
            send(src_all.at[origin], src_all.at[origin], (sa1, ra1), d_next, partner).start()

        send(src, src_all.at[tile * 2 + 1 - core], (sa1, ra1), d, partner).wait_recv()
        rows = src_all[pl.ds(tile * 2, 2)].reshape(TILE, D)
        k_tile = nn(rows, wk[...]).astype(BF16)
        k_scr[tile] = k_tile
        v_scr[tile] = nn(rows, wv[...]).astype(BF16)
        vt_scr[tile] = nt(wvt, rows).astype(BF16)
        for head in range(HEADS):
            keys = jnp.where(own_lanes(TILE, head), k_tile[:, group_cols(head)], key_extra(tile, head).astype(BF16))
            kh[tile, head] = keys
            t = nt(qs[head], keys) * UNIT
            t_scr[tile, head] = t
            rm[head] = jnp.maximum(rm[head], jnp.maximum(t[:, :BLOCK], t[:, BLOCK:]))
            peak = t.max(axis=0, keepdims=True)
            total = jnp.exp2(t - peak).sum(axis=0, keepdims=True)
            lse = peak + jnp.log2(total)
            for kb in range(2):
                lc_part[tile, kb, head : head + 1, :] = lse[:, kb * BLOCK : (kb + 1) * BLOCK]
        swap_columns(tile, lc_part, lc_swap, (sl0, rl0)).start()

        @pl.when(step > 0)
        def _():
            before = from_offset(near_first(step - 1))
            spread_columns(before, log_sum, lc_part, lc_swap, lc_chip, lc_in, (sl0, rl0), (sl1, rl1))

    spread_columns(
        from_offset(4), log_sum, lc_part, lc_swap, lc_chip, lc_in, (sl0, rl0), (sl1, rl1)
    )

    for head in range(HEADS):
        peak = rm[head].max(axis=1, keepdims=True)
        rm[head] = jnp.zeros((ROWS, BLOCK), F32)

        @pl.loop(0, TILES)
        def _(tile):
            rm[head] += jnp.exp2(t_scr[tile, head, :, :BLOCK] - peak) + jnp.exp2(t_scr[tile, head, :, BLOCK:] - peak)

        total = rm[head].sum(axis=1, keepdims=True)
        row_term = peak + jnp.log2(total)
        lr[head] = jnp.broadcast_to(row_term, (ROWS, BLOCK))
        extra = query_extra(inter, head, in_three(row_term * (-1.0 / UNIT))).astype(BF16)
        part = qs[head]
        mask = own_lanes(ROWS, head)
        qb_scr[head] = jnp.where(mask, part, extra)
        qf[head] = jnp.where(mask, part + part, extra)

    att[...] = jnp.zeros_like(att)
    wvg[...] = jnp.zeros_like(wvg)

    @pl.loop(0, TILES)
    def _(tile):
        collect_columns(tile, log_sum, lc_chip, lc_in, lc_all, (sl1, rl1))
        rows = src_all[pl.ds(tile * 2, 2)].reshape(TILE, D)
        for head in range(HEADS):
            lc_row = jnp.concatenate([lc_all[tile, kb, head : head + 1, :] for kb in range(2)], axis=1)
            match = jnp.exp2(nt(qf[head], kh[tile, head]) * UNIT - lc_row).astype(BF16)
            att[head] += by_halves(match, v_scr[tile, :, group_cols(head)])
            gvt = nn(gat_scr[head_lanes(head), :], match)
            gvt_scr[tile, head_lanes(head), :] = gvt.astype(BF16)
            dots = (gvt * vt_scr[tile, head_lanes(head), :].astype(F32)).sum(axis=0, keepdims=True)
            for kb in range(2):
                cd_part[tile, kb, head : head + 1, :] = dots[:, kb * BLOCK : (kb + 1) * BLOCK]
        swap_columns(tile, cd_part, cd_swap, (sc0, rc0)).start()
        wvg[...] += nn(gvt_scr[tile], rows)

        @pl.when(tile > 0)
        def _():
            spread_columns(tile - 1, plain_sum, cd_part, cd_swap, cd_chip, cd_in, (sc0, rc0), (sc1, rc1))

    spread_columns(TILES - 1, plain_sum, cd_part, cd_swap, cd_chip, cd_in, (sc0, rc0), (sc1, rc1))

    for head in range(HEADS):
        mask = own_lanes(ROWS, head)
        value = jnp.where(mask, att[head], 0.0)
        rd = (value * gam[head].astype(F32)).sum(axis=1, keepdims=True)
        rd_scr[head] = jnp.broadcast_to(rd, (ROWS, BLOCK))
        if head % 2 == 0:
            att_all[:, group_cols(head)] = value.astype(BF16)
        else:
            att_all[:, group_cols(head)] = jnp.where(mask, value.astype(BF16), att_all[:, group_cols(head)])
        gam[head] = gam[head] + gam[head]
    matched_out[...] = (ref[...].astype(F32) + nn(att_all[...], wo[...])).astype(BF16)
    pack_weight(wg, 1, 1, nn(att_all[...].T, gout[...]))
    pack_weight(wg, 1, 0, wvg[...].T)
    gq[...] = jnp.zeros_like(gq)
    wkg[...] = jnp.zeros_like(wkg)

    def spread_source(d):
        tile = to_offset(d)
        send(gs_part.at[tile, core], gs_swap.at[tile], (sg0, rg0), tile, partner).wait_recv()
        gs_sum[tile] = (gs_part[tile, core].astype(F32) + gs_swap[tile].astype(F32)).astype(BF16)

    def source_copy(d):
        return send(gs_sum.at[to_offset(d)], gs_in.at[d - 1], (sg1, rg1), d, on_chip(d, core))

    @pl.loop(0, TILES)
    def _(step):
        d = far_first(step)
        tile = to_offset(d)
        collect_columns(tile, plain_sum, cd_chip, cd_in, cd_all, (sc1, rc1))
        rows = src_all[pl.ds(tile * 2, 2)].reshape(TILE, D)
        gk_heads = []
        for head in range(HEADS):
            cols = group_cols(head)
            x = nt(qb_scr[head], kh[tile, head])
            gp = nt(gam[head], v_scr[tile, :, cols])
            lines = []
            for kb in range(2):
                lanes = slice(kb * BLOCK, (kb + 1) * BLOCK)
                lc_row = lc_all[tile, kb, head : head + 1, :]
                cd_row = cd_all[tile, kb, head : head + 1, :]
                u = x[:, lanes] * UNIT
                r = jnp.exp2(u)
                c = jnp.exp2(u + lr[head] - lc_row)
                match = (r * c).astype(BF16).astype(F32)
                lines.append((match * gp[:, lanes] - r * rd_scr[head] - c * cd_row).astype(BF16))
            gs = jnp.concatenate(lines, axis=1)
            gq[head] += by_halves(gs, k_scr[tile, :, cols])
            gk_heads.append((nn(qt_all[head_lanes(head), :], gs) * SCALE).astype(BF16))
        gkt = jnp.concatenate(gk_heads, axis=0)
        wkg[...] += nn(gkt, rows)
        gst = nn(wk[...], gkt) + nn(wv[...], gvt_scr[tile])
        for kb in range(2):
            gs_part[tile, kb] = gst[:, kb * BLOCK : (kb + 1) * BLOCK].astype(BF16)
        send(gs_part.at[tile, 1 - core], gs_swap.at[tile], (sg0, rg0), tile, partner).start()

        @pl.when(step > 0)
        def _():
            d_before = far_first(step - 1)
            spread_source(d_before)
            source_copy(d_before).start()

    for head in range(HEADS):
        mask = own_lanes(ROWS, head)
        value = (gq[head] * SCALE).astype(BF16)
        if head % 2 == 0:
            gq_all[:, group_cols(head)] = value
        else:
            gq_all[:, group_cols(head)] = jnp.where(mask, value, gq_all[:, group_cols(head)])
    pack_weight(wg, 0, 0, nn(ref[...].T, gq_all[...]))
    pack_weight(wg, 0, 1, wkg[...].T)

    copies = []

    def start(*args):
        copy = send(*args)
        copy.start()
        copies.append(copy)
        return copy

    swap = start(wg.at[1 - core], w_swap, (sp, rp), 0, partner)
    gref_out[...] = (gout[...].astype(F32) + nt(gq_all[...], wq[...])).astype(BF16)
    swap.wait_recv()
    w_sum[...] = (wg[core].astype(F32) + w_swap[...].astype(F32)).astype(BF16)
    arrivals = []
    for d in range(1, PLANE):
        arrivals.append(start(w_sum.at[lax.rem(scan + d, PLANE)], w_in.at[d - 1], (sx, rx), d - 1, plane[d - 1]))
    spread_source(0)
    for copy in arrivals:
        copy.wait_recv()
    total = w_sum[scan].astype(F32)
    for d in range(PLANE - 1):
        total = total + w_in[d].astype(F32)
    w_part[...] = total.reshape(CHIPS, 8, BLOCK)
    arrivals = []
    for d in range(1, CHIPS):
        arrivals.append(start(w_part.at[to_offset(d)], z_in.at[d - 1], (sz, rz), d - 1, on_chip(d, core)))
    for copy in arrivals:
        copy.wait_recv()
    total = w_part[chip]
    for d in range(CHIPS - 1):
        total = total + z_in[d]
    w_done[...] = total
    arrivals = []
    for d in range(1, CHIPS):
        arrivals.append(start(w_done, z_all.at[chip], (sy, ry), d - 1, on_chip(d, core)))
    z_all[chip] = total
    for d in (4, 3, 5, 2, 6, 1, 7):
        source_copy(d).wait_recv()
    gsrc = gs_sum[chip].astype(F32)
    for d in range(CHIPS - 1):
        gsrc = gsrc + gs_in[d].astype(F32)
    gsrc_out[...] = gsrc.T.astype(BF16)
    for copy in arrivals:
        copy.wait_recv()
    row = z_all[...].reshape(CHIPS * 8, BLOCK).astype(BF16)
    w_row[...] = row
    arrivals = []
    for d in range(1, PLANE):
        arrivals.append(start(w_row, w_all.at[core, scan], (sb, rb), d - 1, plane[d - 1]))
    w_all[core, scan] = row
    for copy in arrivals:
        copy.wait_recv()
    start(w_all.at[core], w_all.at[core], (sp, rp), 1, partner).wait_recv()
    for core_at, pair in enumerate(((wq_out, wk_out), (wv_out, wo_out))):
        for which, out in enumerate(pair):
            for half in range(2):
                for part in range(4):
                    out[64 * part : 64 * (part + 1), half * BLOCK : (half + 1) * BLOCK] = w_all[
                        core_at, 4 * (2 * which + half) + part
                    ].astype(F32)

    for copy in copies:
        copy.wait_send()

    @pl.loop(0, TILES)
    def _(tile):
        send(src, src_all.at[blk], (sa1, ra1), tile, partner).wait_send()
        swap_columns(tile, lc_part, lc_swap, (sl0, rl0)).wait_send()
        swap_columns(tile, cd_part, cd_swap, (sc0, rc0)).wait_send()
        send(lc_in.at[tile], lc_in.at[tile], (sl1, rl1), tile, partner).wait_send()
        send(cd_in.at[tile], cd_in.at[tile], (sc1, rc1), tile, partner).wait_send()
        send(gs_part.at[tile, core], gs_swap.at[tile], (sg0, rg0), tile, partner).wait_send()

        @pl.when(tile > 0)
        def _():
            send(src, src_all.at[blk], (sa0, ra0), tile, partner).wait_send()
            send(gs_sum.at[tile], gs_in.at[0], (sg1, rg1), tile, partner).wait_send()


def shape(dims, dtype):
    return jax.ShapeDtypeStruct(dims, dtype)


def layer(ref, gout, src, wq, wk, wv, wo, inter):
    vm = pltpu.VMEM
    row = (64, BLOCK)
    heads = (HEADS, ROWS, BLOCK)
    pair = (TILES, 2, HEADS, BLOCK)
    columns = [vm(pair, F32), vm(pair, F32), vm(pair, F32), vm((TILES, CHIPS - 1, 2, HEADS, BLOCK), F32), vm(pair, F32)]
    scratch = [
        vm((2 * CHIPS, BLOCK, D), BF16), vm((TILES, TILE, D), BF16), vm((TILES, HEADS, TILE, BLOCK), BF16),
        vm((TILES, TILE, D), BF16), vm((TILES, D, TILE), BF16), vm(heads, BF16), vm(heads, BF16), vm(heads, BF16),
        vm(heads, BF16), vm((D, ROWS), BF16), vm((D, ROWS), BF16), vm((TILES, HEADS, ROWS, TILE), F32), vm(heads, F32), vm(heads, F32),
        *columns, *columns,
        vm(heads, F32), vm((ROWS, D), BF16), vm((TILES, D, TILE), BF16), vm(heads, F32), vm((D, D), F32),
        vm((D, D), F32), vm(heads, F32), vm((ROWS, D), BF16),
        vm((TILES, 2, D, BLOCK), BF16), vm((TILES, D, BLOCK), BF16), vm((TILES, D, BLOCK), BF16),
        vm((CHIPS - 1, D, BLOCK), BF16),
        vm((2, PLANE) + row, BF16), vm((PLANE,) + row, BF16), vm((PLANE,) + row, BF16), vm((PLANE - 1,) + row, BF16),
        vm((CHIPS, 8, BLOCK), F32), vm((CHIPS - 1, 8, BLOCK), F32), vm((8, BLOCK), F32), vm((CHIPS, 8, BLOCK), F32),
        vm(row, BF16), vm((2, PLANE) + row, BF16),
        DMA,
    ] + [DMA((n,)) for n in (8,) * 16 + (2, 2, 15, 15, 7, 7, 7, 7, 15, 15)]
    return pl.pallas_call(
        layer_kernel,
        out_shape=[shape((ROWS, D), BF16)] * 2 + [shape((BLOCK, D), BF16)] + [shape((D, D), F32)] * 4,
        in_specs=[VMEM] * 7 + [SMEM],
        out_specs=[VMEM] * 7,
        scratch_shapes=scratch,
        compiler_params=pltpu.CompilerParams(vmem_limit_bytes=60 << 20, collective_id=1, has_side_effects=True),
        name="layer",
    )(ref, gout, src, wq, wk, wv, wo, inter)


def on_device(ref_feats, src_feats, grad_out, w_query, w_key, w_value, w_out, intersection):
    matched, gref, gsrc, wqg, wkg, wvg, wog = layer(
        ref_feats[0], grad_out[0], src_feats[0], w_query, w_key, w_value, w_out, intersection[0]
    )
    return matched[None], gref[None], gsrc[None], wqg, wkg, wvg, wog


def solution(mesh):
    split = P("scan", "blk", None)
    return jax.shard_map(
        on_device, mesh=mesh,
        in_specs=(split, split, split, P(), P(), P(), P(), split),
        out_specs=(split, split, split, P(), P(), P(), P()),
        check_vma=False,
    )
```

time: 648 us -> 106 us (0.16)
  waiting for transfers between devices: 355 us -> 0 us
  Pallas kernels: 0 us -> 97.6 us
  matrix products: 91.2 us -> 0 us
  blocking collectives: 77.3 us -> 0 us
  local copies, waits for them, and re-layouts: 58.9 us -> 7.04 us
  other arithmetic: 46.1 us -> 0 us
  between operations: 13.9 us -> 0.66 us
    psum x1 -> x0, waiting for transfers between devices: 258 us -> none  [on_device(): lax.psum((weight_query, weight_key, weight_value, weight_out), ('scan', '...]
    pallas_call x0 -> x1, Pallas kernels: none -> 97.6 us  [layer(): pl.pallas_call(layer_kernel, out_shape=[shape((ROWS, D), BF16)] * 2 + [sh...]
    dot_general x48 -> x0, matrix products: 91.2 us -> none  [the longest x12 24.4 us: raw_scores(): jnp.einsum('ihc,jhc->hij', query_heads, key_heads(first_row, tile_rows),...]
    unnamed x4 -> x0, waiting for transfers between devices: 57.9 us -> none
    psum x1 -> x0, blocking collectives: 44 us -> none  [on_device(): col_dot = lax.psum(col_dot, 'blk')]
    all_gather x1 -> x0, waiting for transfers between devices: 39.3 us -> none  [on_device(): lax.all_gather(jnp.concatenate([key_local, value_local], axis=1), 'blk',...]
    dynamic_slice x46 -> x0, local copies, waits for them, and re-layouts: 36.8 us -> none  [the longest x12 8.3 us: mask_blocks(): lax.dynamic_slice_in_dim(blocks, first_row // BLOCK, tile_rows // BLOCK, 1)]
    all_gather x2 -> x0, blocking collectives: 33.2 us -> none  [combined_all(): gathered = jax.tree.map(lambda a: lax.all_gather(a, axis), part)]
  transfers between devices with their start and end apart: 3 -> 0, of which waited for: 3 -> 0; matrix products, arithmetic and copies ran while one was open for 2% -> 0% of each run, Pallas kernels for 0% -> 0%
where the time goes in v2:
time: 106 us; the launch traced here: 105 us
  Pallas kernels  97.6 us (92%)
  local copies, waits for them, and re-layouts  7.04 us (7%)
    pallas_call x1, Pallas kernels, layer(): pl.pallas_call(layer_kernel, out_shape=[shape((ROWS, D), BF16)] * 2 + [sh...  97.6 us
    unnamed x19, local copies, waits for them, and re-layouts  7.04 us

profile of v2, /device:TPU:1, one launch (start us, length us, event | category | flops | bytes accessed | tf_op | source)
XLA Modules:
  0.0 105.3 jit_solution(13664406218599425582)
XLA Ops:
  0.6 97.6 %layer.1 = (bf16[512,256]{1,0:T(8,128)(2,1)}, bf16[512,256]{1,0:T(8,128)(2,1)}, bf16[128,256]{1,0:T(8,128)(2,1)}, f32[256,256]{1,0:T(8,128)}, f32[256,256]{1,0:T...) custom-call(bf16[512,256]{1,0:T(8,128)(2,1)} %bitcast.7, bf16[512,256]{1,0:T(8,128)(2,1)} %bitcast.8, ...), custom_call_target="tpu_custom_call" | custom-call | tf_op jit(solution)/shard_map/layer/pallas_call | solution.py:457
  98.2 0.0 copy-start.4
  98.3 1.7 %copy.22 = bf16[1,512,256]{2,1,0:T(8,128)(2,1)} copy(bf16[1,512,256]{2,1,0:T(8,128)(2,1)} %bitcast.10) | data formatting | bytes 524288
  100.0 0.0 copy-done.4
  100.0 0.0 copy-start.5
  100.0 0.0 copy-start.3
  100.0 0.7 copy.23
  100.7 0.2 copy-done.5
  100.8 0.6 copy.24
  101.5 0.0 copy-done.3
  101.5 0.0 copy-start.2
  101.5 0.7 copy.25
  102.2 0.3 copy-done.2
  102.5 0.0 copy-start.1
  102.5 0.7 copy.26
  103.2 0.3 copy-done.1
  103.6 0.0 copy-start
  103.6 0.7 copy.27
  104.3 0.3 copy-done
  104.6 0.7 copy.28
Async XLA Ops:
  98.2 1.7 %copy-start.4 = (bf16[512,256]{1,0:T(8,128)(2,1)S(1)}, bf16[512,256]{1,0:T(8,128)(2,1)}, u32[]{:S(2)}) copy-start(bf16[512,256]{1,0:T(8,128)(2,1)} %get-tuple-element.15) | copy-start | bytes 786436
  100.0 0.9 copy-start.5
  100.0 1.5 %copy-start.3 = (f32[256,256]{1,0:T(8,128)S(1)}, f32[256,256]{1,0:T(8,128)}, u32[]{:S(2)}) copy-start(f32[256,256]{1,0:T(8,128)} %get-tuple-element.31) | copy-start | bytes 786436
  101.5 1.0 copy-start.2
  102.5 1.0 copy-start.1
  103.6 1.0 copy-start

commit v3 on v2

--- a/solution.py
+++ b/solution.py
@@ -20,6 +20,8 @@
 KBLOCKS = KEYS // BLOCK
 CHIPS = 8
 PLANE = 16
+CHUNK = 32
+PIECE = CHUNK // CHIPS
 NEG = -1.0e30
 SCALE = HEAD_DIM**-0.5
 UNIT = SCALE * math.log2(math.e)
@@ -108,12 +110,20 @@
     return sum(parts)
 
 
-def pack_weight(wg, core, which, matrix):
+def pack_weight(wg, core, matrix):
     for half in range(2):
-        for part in range(4):
-            wg[core, 4 * (2 * which + half) + part] = matrix[
-                64 * part : 64 * (part + 1), half * BLOCK : (half + 1) * BLOCK
+        for part in range(8):
+            wg[core, 8 * half + part] = matrix[
+                CHUNK * part : CHUNK * (part + 1), half * BLOCK : (half + 1) * BLOCK
             ].astype(BF16)
+
+
+def unpack_weight(out, packed, core):
+    for half in range(2):
+        for part in range(8):
+            out[CHUNK * part : CHUNK * (part + 1), half * BLOCK : (half + 1) * BLOCK] = packed[
+                core, 8 * half + part
+            ].astype(F32)
 
 
 def send(src, dst, sems, index, target):
@@ -125,14 +135,15 @@
 
 def layer_kernel(
     ref, gout, src, wq, wk, wv, wo, inter,
-    matched_out, gref_out, gsrc_out, wq_out, wk_out, wv_out, wo_out,
+    matched_out, gref_out, gsrc_out, early_out, late_out,
     src_all, k_scr, kh, v_scr, vt_scr, qs, qf, qb_scr, gam, gat_scr, qt_all, t_scr, rm, lr,
     lc_part, lc_swap, lc_chip, lc_in, lc_all, cd_part, cd_swap, cd_chip, cd_in, cd_all,
     att, att_all, gvt_scr, rd_scr, wvg, wkg, gq, gq_all,
-    gs_part, gs_swap, gs_sum, gs_in, wg, w_swap, w_sum, w_in, w_part, z_in, w_done, z_all, w_row, w_all,
-    own_sem, sa0, ra0, sa1, ra1, sl0, rl0, sl1, rl1, sc0, rc0, sc1, rc1, sg0, rg0, sg1, rg1,
-    sp, rp, sx, rx, sz, rz, sy, ry, sb, rb,
+    gs_part, gs_swap, gs_sum, gs_in, *rest,
 ):
+    early_bufs, late_bufs, rest = rest[:10], rest[10:20], rest[20:]
+    own_sem, sa0, ra0, sa1, ra1, sl0, rl0, sl1, rl1, sc0, rc0, sc1, rc1, sg0, rg0, sg1, rg1 = rest[:17]
+    early_sems, late_sems = rest[17:27], rest[27:37]
     blk = lax.axis_index("blk")
     scan = lax.axis_index("scan")
     chip = lax.div(blk, 2)
@@ -141,6 +152,34 @@
 
     def on_chip(offset, core_at):
         return {"blk": lax.rem(chip + offset, CHIPS) * 2 + core_at}
+
+    def from_offset(d):
+        return lax.rem(chip + CHIPS - d, CHIPS)
+
+    def to_offset(d):
+        return lax.rem(chip + d, CHIPS)
+
+    def ring_copy(block, way, hops, piece, source=None):
+        rows = pl.ds(piece * (BLOCK // 2), BLOCK // 2)
+        landing = src_all.at[block, rows]
+        return send(
+            landing if source is None else source.at[rows], landing, (sa0, ra0),
+            way * 8 + (hops - 1) * 2 + piece, on_chip(1 if way == 0 else CHIPS - 1, core),
+        )
+
+    def pieces_of(way, hops):
+        return range(2) if hops < 4 else (way,)
+
+    def relay(hops):
+        for way in range(2):
+            origin = from_offset(hops if way == 0 else CHIPS - hops) * 2 + core
+            for piece in pieces_of(way, hops):
+                ring_copy(origin, way, hops, piece).wait_recv()
+                if hops < 4 and piece in pieces_of(way, hops + 1):
+                    ring_copy(origin, way, hops + 1, piece).start()
+        for d in (hops, CHIPS - hops) if hops < 4 else (hops,):
+            origin = from_offset(d) * 2 + core
+            send(src_all.at[origin], src_all.at[origin], (sa1, ra1), d, partner).start()
 
     plane = [{"scan": lax.rem(scan + d, PLANE)} for d in range(1, PLANE)]
     column = [on_chip(d, c) for d in range(1, CHIPS) for c in range(2)]
@@ -148,6 +187,77 @@
     everyone = [partner] + column + plane
     for target in everyone:
         pl.semaphore_signal(barrier, inc=1, device_id=target, device_id_type=MESH)
+
+    def all_reduce(bufs, sems):
+        wg, w_swap, w_sum, w_in, w_part, z_in, w_done, z_all, w_row, w_all = bufs
+        swap_sems, in_sems, z_sems, back_sems, out_sems = [sems[2 * i : 2 * i + 2] for i in range(5)]
+        swap = [
+            send(wg.at[1 - core], w_swap, swap_sems, 0, partner),
+            send(w_all.at[core], w_all.at[core], swap_sems, 1, partner),
+        ]
+
+        def in_plane(d):
+            return send(w_sum.at[lax.rem(scan + d, PLANE)], w_in.at[d - 1], in_sems, d - 1, plane[d - 1])
+
+        def in_column(d):
+            return send(w_part.at[to_offset(d)], z_in.at[d - 1], z_sems, d - 1, on_chip(d, core))
+
+        def back_column(d):
+            return send(w_done, z_all.at[chip], back_sems, d - 1, on_chip(d, core))
+
+        def back_plane(d):
+            return send(w_row, w_all.at[core, scan], out_sems, d - 1, plane[d - 1])
+
+        def stage_1():
+            swap[0].wait_recv()
+            w_sum[...] = (wg[core].astype(F32) + w_swap[...].astype(F32)).astype(BF16)
+            for d in range(1, PLANE):
+                in_plane(d).start()
+
+        def stage_2():
+            for d in range(1, PLANE):
+                in_plane(d).wait_recv()
+            total = w_sum[scan].astype(F32)
+            for d in range(PLANE - 1):
+                total = total + w_in[d].astype(F32)
+            for c in range(CHIPS):
+                w_part[c] = total[c * PIECE : (c + 1) * PIECE, :]
+            for d in range(1, CHIPS):
+                in_column(d).start()
+
+        def stage_3():
+            for d in range(1, CHIPS):
+                in_column(d).wait_recv()
+            total = w_part[chip]
+            for d in range(CHIPS - 1):
+                total = total + z_in[d]
+            w_done[...] = total
+            z_all[chip] = total
+            for d in range(1, CHIPS):
+                back_column(d).start()
+
+        def stage_4():
+            for d in range(1, CHIPS):
+                back_column(d).wait_recv()
+            row = jnp.concatenate([z_all[c] for c in range(CHIPS)], axis=0).astype(BF16)
+            w_row[...] = row
+            w_all[core, scan] = row
+            for d in range(1, PLANE):
+                back_plane(d).start()
+
+        def stage_5():
+            for d in range(1, PLANE):
+                back_plane(d).wait_recv()
+            swap[1].start()
+
+        def left():
+            for copy in swap:
+                copy.wait_send()
+            for make, count in ((in_plane, PLANE), (in_column, CHIPS), (back_column, CHIPS), (back_plane, PLANE)):
+                for d in range(1, count):
+                    make(d).wait_send()
+
+        return swap[0].start, stage_1, stage_2, stage_3, stage_4, stage_5, swap[1].wait_recv, left
 
     q_rows = nn(ref[...], wq[...]).astype(BF16)
     for head in range(HEADS):
@@ -160,8 +270,9 @@
     own.start()
 
     pl.semaphore_wait(barrier, len(everyone))
-    for d in (4, 3, 5, 2, 6, 1, 7):
-        send(src, src_all.at[blk], (sa0, ra0), d, on_chip(d, core)).start()
+    for piece in range(2):
+        for way in range(2):
+            ring_copy(blk, way, 1, piece, src).start()
     send(src, src_all.at[blk], (sa1, ra1), 0, partner).start()
 
     ga_rows = nt(gout[...], wo[...]).astype(BF16)
@@ -176,14 +287,8 @@
         half = lax.div(step + 1, 2)
         return jnp.where(lax.rem(step, 2) == 1, half, lax.rem(CHIPS - half, CHIPS))
 
-    def far_first(step):
-        return jnp.where(lax.rem(step, 2) == 0, 4 + lax.div(step, 2), 4 - lax.div(step + 1, 2))
-
-    def from_offset(d):
-        return lax.rem(chip + CHIPS - d, CHIPS)
-
-    def to_offset(d):
-        return lax.rem(chip + d, CHIPS)
+    def by_quarters(step):
+        return lax.div(step, 4) * 4 + lax.rem(chip + 1 + step, 4)
 
     def swap_columns(tile, part, swap, sems):
         return send(part.at[tile], swap.at[tile], sems, tile, partner)
@@ -204,12 +309,11 @@
         d = near_first(step)
         tile = from_offset(d)
 
-        @pl.when(step < TILES - 1)
-        def _():
-            d_next = near_first(step + 1)
-            origin = from_offset(d_next) * 2 + core
-            send(src, src_all.at[origin], (sa0, ra0), d_next, partner).wait_recv()
-            send(src_all.at[origin], src_all.at[origin], (sa1, ra1), d_next, partner).start()
+        for at, hops in ((1, 1), (2, 2), (4, 3), (6, 4)):
+
+            @pl.when(step == at)
+            def _():
+                relay(hops)
 
         send(src, src_all.at[tile * 2 + 1 - core], (sa1, ra1), d, partner).wait_recv()
         rows = src_all[pl.ds(tile * 2, 2)].reshape(TILE, D)
@@ -292,23 +396,34 @@
             att_all[:, group_cols(head)] = jnp.where(mask, value.astype(BF16), att_all[:, group_cols(head)])
         gam[head] = gam[head] + gam[head]
     matched_out[...] = (ref[...].astype(F32) + nn(att_all[...], wo[...])).astype(BF16)
-    pack_weight(wg, 1, 1, nn(att_all[...].T, gout[...]))
-    pack_weight(wg, 1, 0, wvg[...].T)
+    pack_weight(early_bufs[0], 1, nn(att_all[...].T, gout[...]))
+    pack_weight(early_bufs[0], 0, wvg[...].T)
+    early = all_reduce(early_bufs, early_sems)
+    early[0]()
     gq[...] = jnp.zeros_like(gq)
     wkg[...] = jnp.zeros_like(wkg)
 
-    def spread_source(d):
-        tile = to_offset(d)
+    def source_copy(d):
+        return send(gs_sum.at[to_offset(d)], gs_in.at[d - 1], (sg1, rg1), d, on_chip(d, core))
+
+    def spread_source(tile):
         send(gs_part.at[tile, core], gs_swap.at[tile], (sg0, rg0), tile, partner).wait_recv()
         gs_sum[tile] = (gs_part[tile, core].astype(F32) + gs_swap[tile].astype(F32)).astype(BF16)
-
-    def source_copy(d):
-        return send(gs_sum.at[to_offset(d)], gs_in.at[d - 1], (sg1, rg1), d, on_chip(d, core))
+        d = lax.rem(tile + CHIPS - chip, CHIPS)
+
+        @pl.when(d > 0)
+        def _():
+            source_copy(d).start()
 
     @pl.loop(0, TILES)
     def _(step):
-        d = far_first(step)
-        tile = to_offset(d)
+        tile = by_quarters(step)
+        for at, stage in ((1, 1), (3, 2), (6, 3)):
+
+            @pl.when(step == at)
+            def _():
+                early[stage]()
+
         collect_columns(tile, plain_sum, cd_chip, cd_in, cd_all, (sc1, rc1))
         rows = src_all[pl.ds(tile * 2, 2)].reshape(TILE, D)
         gk_heads = []
@@ -338,9 +453,7 @@
 
         @pl.when(step > 0)
         def _():
-            d_before = far_first(step - 1)
-            spread_source(d_before)
-            source_copy(d_before).start()
+            spread_source(by_quarters(step - 1))
 
     for head in range(HEADS):
         mask = own_lanes(ROWS, head)
@@ -349,71 +462,36 @@
             gq_all[:, group_cols(head)] = value
         else:
             gq_all[:, group_cols(head)] = jnp.where(mask, value, gq_all[:, group_cols(head)])
-    pack_weight(wg, 0, 0, nn(ref[...].T, gq_all[...]))
-    pack_weight(wg, 0, 1, wkg[...].T)
-
-    copies = []
-
-    def start(*args):
-        copy = send(*args)
-        copy.start()
-        copies.append(copy)
-        return copy
-
-    swap = start(wg.at[1 - core], w_swap, (sp, rp), 0, partner)
+    pack_weight(late_bufs[0], 0, nn(ref[...].T, gq_all[...]))
+    pack_weight(late_bufs[0], 1, wkg[...].T)
+    late = all_reduce(late_bufs, late_sems)
+    late[0]()
+    early[4]()
     gref_out[...] = (gout[...].astype(F32) + nt(gq_all[...], wq[...])).astype(BF16)
-    swap.wait_recv()
-    w_sum[...] = (wg[core].astype(F32) + w_swap[...].astype(F32)).astype(BF16)
-    arrivals = []
-    for d in range(1, PLANE):
-        arrivals.append(start(w_sum.at[lax.rem(scan + d, PLANE)], w_in.at[d - 1], (sx, rx), d - 1, plane[d - 1]))
-    spread_source(0)
-    for copy in arrivals:
-        copy.wait_recv()
-    total = w_sum[scan].astype(F32)
-    for d in range(PLANE - 1):
-        total = total + w_in[d].astype(F32)
-    w_part[...] = total.reshape(CHIPS, 8, BLOCK)
-    arrivals = []
-    for d in range(1, CHIPS):
-        arrivals.append(start(w_part.at[to_offset(d)], z_in.at[d - 1], (sz, rz), d - 1, on_chip(d, core)))
-    for copy in arrivals:
-        copy.wait_recv()
-    total = w_part[chip]
-    for d in range(CHIPS - 1):
-        total = total + z_in[d]
-    w_done[...] = total
-    arrivals = []
-    for d in range(1, CHIPS):
-        arrivals.append(start(w_done, z_all.at[chip], (sy, ry), d - 1, on_chip(d, core)))
-    z_all[chip] = total
+    late[1]()
+    spread_source(by_quarters(TILES - 1))
+    early[5]()
+    late[2]()
+    late[3]()
     for d in (4, 3, 5, 2, 6, 1, 7):
         source_copy(d).wait_recv()
     gsrc = gs_sum[chip].astype(F32)
     for d in range(CHIPS - 1):
         gsrc = gsrc + gs_in[d].astype(F32)
     gsrc_out[...] = gsrc.T.astype(BF16)
-    for copy in arrivals:
-        copy.wait_recv()
-    row = z_all[...].reshape(CHIPS * 8, BLOCK).astype(BF16)
-    w_row[...] = row
-    arrivals = []
-    for d in range(1, PLANE):
-        arrivals.append(start(w_row, w_all.at[core, scan], (sb, rb), d - 1, plane[d - 1]))
-    w_all[core, scan] = row
-    for copy in arrivals:
-        copy.wait_recv()
-    start(w_all.at[core], w_all.at[core], (sp, rp), 1, partner).wait_recv()
-    for core_at, pair in enumerate(((wq_out, wk_out), (wv_out, wo_out))):
-        for which, out in enumerate(pair):
-            for half in range(2):
-                for part in range(4):
-                    out[64 * part : 64 * (part + 1), half * BLOCK : (half + 1) * BLOCK] = w_all[
-                        core_at, 4 * (2 * which + half) + part
-                    ].astype(F32)
-
-    for copy in copies:
-        copy.wait_send()
+    early[6]()
+    early_out[...] = early_bufs[-1][...]
+    late[4]()
+    late[5]()
+    late[6]()
+    late_out[...] = late_bufs[-1][...]
+
+    early[7]()
+    late[7]()
+    for way in range(2):
+        for hops in range(1, 5):
+            for piece in pieces_of(way, hops):
+                ring_copy(blk, way, hops, piece).wait_send()
 
     @pl.loop(0, TILES)
     def _(tile):
@@ -426,7 +504,6 @@
 
         @pl.when(tile > 0)
         def _():
-            send(src, src_all.at[blk], (sa0, ra0), tile, partner).wait_send()
             send(gs_sum.at[tile], gs_in.at[0], (sg1, rg1), tile, partner).wait_send()
 
 
@@ -436,7 +513,12 @@
 
 def layer(ref, gout, src, wq, wk, wv, wo, inter):
     vm = pltpu.VMEM
-    row = (64, BLOCK)
+    row = (CHUNK, BLOCK)
+    reduction = [
+        vm((2, PLANE) + row, BF16), vm((PLANE,) + row, BF16), vm((PLANE,) + row, BF16), vm((PLANE - 1,) + row, BF16),
+        vm((CHIPS, PIECE, BLOCK), F32), vm((CHIPS - 1, PIECE, BLOCK), F32), vm((PIECE, BLOCK), F32),
+        vm((CHIPS, PIECE, BLOCK), F32), vm(row, BF16), vm((2, PLANE) + row, BF16),
+    ]
     heads = (HEADS, ROWS, BLOCK)
     pair = (TILES, 2, HEADS, BLOCK)
     columns = [vm(pair, F32), vm(pair, F32), vm(pair, F32), vm((TILES, CHIPS - 1, 2, HEADS, BLOCK), F32), vm(pair, F32)]
@@ -449,26 +531,44 @@
         vm((D, D), F32), vm(heads, F32), vm((ROWS, D), BF16),
         vm((TILES, 2, D, BLOCK), BF16), vm((TILES, D, BLOCK), BF16), vm((TILES, D, BLOCK), BF16),
         vm((CHIPS - 1, D, BLOCK), BF16),
-        vm((2, PLANE) + row, BF16), vm((PLANE,) + row, BF16), vm((PLANE,) + row, BF16), vm((PLANE - 1,) + row, BF16),
-        vm((CHIPS, 8, BLOCK), F32), vm((CHIPS - 1, 8, BLOCK), F32), vm((8, BLOCK), F32), vm((CHIPS, 8, BLOCK), F32),
-        vm(row, BF16), vm((2, PLANE) + row, BF16),
-        DMA,
-    ] + [DMA((n,)) for n in (8,) * 16 + (2, 2, 15, 15, 7, 7, 7, 7, 15, 15)]
+        *reduction, *reduction,
+        DMA, DMA((16,)), DMA((16,)),
+    ] + [DMA((n,)) for n in (8,) * 14 + 2 * (2, 2, 15, 15, 7, 7, 7, 7, 15, 15)]
     return pl.pallas_call(
         layer_kernel,
-        out_shape=[shape((ROWS, D), BF16)] * 2 + [shape((BLOCK, D), BF16)] + [shape((D, D), F32)] * 4,
+        out_shape=[shape((ROWS, D), BF16)] * 2 + [shape((BLOCK, D), BF16)] + [shape((2, PLANE) + row, BF16)] * 2,
         in_specs=[VMEM] * 7 + [SMEM],
-        out_specs=[VMEM] * 7,
+        out_specs=[VMEM] * 5,
         scratch_shapes=scratch,
         compiler_params=pltpu.CompilerParams(vmem_limit_bytes=60 << 20, collective_id=1, has_side_effects=True),
         name="layer",
     )(ref, gout, src, wq, wk, wv, wo, inter)
 
 
+def finish_kernel(matched, gref, gsrc, early, late, matched_out, gref_out, gsrc_out, wq_out, wk_out, wv_out, wo_out):
+    matched_out[...] = matched[...]
+    gref_out[...] = gref[...]
+    gsrc_out[...] = gsrc[...]
+    unpack_weight(wq_out, late, 0)
+    unpack_weight(wk_out, late, 1)
+    unpack_weight(wv_out, early, 0)
+    unpack_weight(wo_out, early, 1)
+
+
+def finish(*parts):
+    return pl.pallas_call(
+        finish_kernel,
+        out_shape=[shape((ROWS, D), BF16)] * 2 + [shape((BLOCK, D), BF16)] + [shape((D, D), F32)] * 4,
+        in_specs=[VMEM] * 5,
+        out_specs=[VMEM] * 7,
+        compiler_params=pltpu.CompilerParams(vmem_limit_bytes=32 << 20),
+        name="finish",
+    )(*parts)
+
+
 def on_device(ref_feats, src_feats, grad_out, w_query, w_key, w_value, w_out, intersection):
-    matched, gref, gsrc, wqg, wkg, wvg, wog = layer(
-        ref_feats[0], grad_out[0], src_feats[0], w_query, w_key, w_value, w_out, intersection[0]
-    )
+    parts = layer(ref_feats[0], grad_out[0], src_feats[0], w_query, w_key, w_value, w_out, intersection[0])
+    matched, gref, gsrc, wqg, wkg, wvg, wog = finish(*parts)
     return matched[None], gref[None], gsrc[None], wqg, wkg, wvg, wog
 
 

time: 106 us -> 101 us (0.953)
  local copies, waits for them, and re-layouts: 7.04 us -> 4.63 us
  Pallas kernels: 97.6 us -> 95.7 us
    pallas_call x1, Pallas kernels: 97.6 us -> 94.4 us  [layer(): pl.pallas_call(layer_kernel, out_shape=[shape((ROWS, D), BF16)] * 2 + [sh...]
    unnamed x19 -> x10, local copies, waits for them, and re-layouts: 7.04 us -> 4.63 us
    pallas_call x0 -> x1, Pallas kernels: none -> 1.25 us  [finish(): pl.pallas_call(finish_kernel, out_shape=[shape((ROWS, D), BF16)] * 2 + [s...]
where the time goes in v3:
time: 101 us
  Pallas kernels  95.7 us (95%)
  local copies, waits for them, and re-layouts  4.63 us (5%)
    pallas_call x1, Pallas kernels, layer(): pl.pallas_call(layer_kernel, out_shape=[shape((ROWS, D), BF16)] * 2 + [sh...  94.4 us
    unnamed x10, local copies, waits for them, and re-layouts  4.63 us

profile of v3, /device:TPU:1, one launch (start us, length us, event | category | flops | bytes accessed | tf_op | source)
XLA Modules:
  0.0 100.9 jit_solution(8122364535687998689)
XLA Ops:
  0.6 94.4 %layer.1 = (bf16[512,256]{1,0:T(8,128)(2,1)}, bf16[512,256]{1,0:T(8,128)(2,1)}, bf16[128,256]{1,0:T(8,128)(2,1)}, bf16[2,16,32,128]{3,2,1,0:T(8,128)(2,1)}, bf16[2,16,32,128]{3,2,1,0:T(8,128)(2,1)}) custom-call(bf16[512,256]{1,0:T(8,128)(2,1)} %bitcast.7, bf16[512,256]{1,0:T(8,128)(2,1)} %bitcast.8, bf16[128,256]{1,0:T(8,128)(2,1)} %bitcast.9, ...), custom_call_target="tpu_custom_call" | custom-call | tf_op jit(solution)/shard_map/layer/pallas_call | solution.py:537
  95.0 0.0 copy-start
  95.1 0.9 copy-done
  96.0 0.0 copy-start.1
  96.0 0.9 copy-done.1
  96.9 0.0 copy-start.2
  96.9 0.9 copy-done.2
  97.9 0.0 copy-start.3
  97.9 0.9 copy-done.3
  98.8 0.0 copy-start.4
  98.8 0.8 copy-done.4
  99.7 1.2 %finish.1 = (bf16[512,256]{1,0:T(8,128)(2,1)}, bf16[512,256]{1,0:T(8,128)(2,1)}, bf16[128,256]{1,0:T(8,128)(2,1)}, f32[256,256]{1,0:T(8,128)}, f32[256,256]{1,0:...) custom-call(bf16[512,256]{1,0:T(8,128)(2,1)S(1)} %copy-done, bf16[512,256]{1,0:T(8,128)(2,1)S(1)} %copy-done.1, ...), custom_call_target="tpu_custom_call" | custom-call | tf_op jit(solution)/shard_map/finish/pallas_call | solution.py:559
Async XLA Ops:
  95.0 1.0 copy-start
  96.0 0.9 copy-start.1
  96.9 0.9 copy-start.2
  97.9 0.9 copy-start.3
  98.8 0.8 copy-start.4

commit v4 on v3

--- a/solution.py
+++ b/solution.py
@@ -21,7 +21,7 @@
 CHIPS = 8
 PLANE = 16
 CHUNK = 32
-PIECE = CHUNK // CHIPS
+OUT_ROWS = 2 * ROWS + BLOCK + 4 * D
 NEG = -1.0e30
 SCALE = HEAD_DIM**-0.5
 UNIT = SCALE * math.log2(math.e)
@@ -39,11 +39,6 @@
 
 def nt(a, b):
     return lax.dot_general(a, b, (((1,), (1,)), ((), ())), preferred_element_type=F32)
-
-
-def by_halves(a, b):
-    half = a.shape[0] // 2
-    return jnp.concatenate([nn(a[:half], b), nn(a[half:], b)], axis=0)
 
 
 def lanes_of(rows):
@@ -118,12 +113,22 @@
             ].astype(BF16)
 
 
-def unpack_weight(out, packed, core):
-    for half in range(2):
-        for part in range(8):
-            out[CHUNK * part : CHUNK * (part + 1), half * BLOCK : (half + 1) * BLOCK] = packed[
-                core, 8 * half + part
-            ].astype(F32)
+def put_weights(out, packed, pair):
+    for core in range(2):
+        first = 2 * ROWS + BLOCK + (2 * pair + core) * D
+        for half in range(2):
+            for part in range(8):
+                out[first + CHUNK * part : first + CHUNK * (part + 1), half * BLOCK : (half + 1) * BLOCK] = packed[
+                    core, 8 * half + part
+                ]
+
+
+def in_turn(make, use):
+    make(0)
+    for head in range(HEADS):
+        if head + 1 < HEADS:
+            make(head + 1)
+        use(head)
 
 
 def send(src, dst, sems, index, target):
@@ -135,15 +140,15 @@
 
 def layer_kernel(
     ref, gout, src, wq, wk, wv, wo, inter,
-    matched_out, gref_out, gsrc_out, early_out, late_out,
-    src_all, k_scr, kh, v_scr, vt_scr, qs, qf, qb_scr, gam, gat_scr, qt_all, t_scr, rm, lr,
+    out,
+    src_all, kt_scr, kh, v_scr, vt_scr, qs, qf, qb_scr, gam, gat_scr, qt_all, t_scr, rm, lr,
     lc_part, lc_swap, lc_chip, lc_in, lc_all, cd_part, cd_swap, cd_chip, cd_in, cd_all,
-    att, att_all, gvt_scr, rd_scr, wvg, wkg, gq, gq_all,
+    att, match_scr, gvt_scr, rd_scr, wvg, wkg, gq,
     gs_part, gs_swap, gs_sum, gs_in, *rest,
 ):
-    early_bufs, late_bufs, rest = rest[:10], rest[10:20], rest[20:]
+    early_bufs, late_bufs, rest = rest[:8], rest[8:16], rest[16:]
     own_sem, sa0, ra0, sa1, ra1, sl0, rl0, sl1, rl1, sc0, rc0, sc1, rc1, sg0, rg0, sg1, rg1 = rest[:17]
-    early_sems, late_sems = rest[17:27], rest[27:37]
+    early_sems, late_sems = rest[17:25], rest[25:33]
     blk = lax.axis_index("blk")
     scan = lax.axis_index("scan")
     chip = lax.div(blk, 2)
@@ -189,8 +194,8 @@
         pl.semaphore_signal(barrier, inc=1, device_id=target, device_id_type=MESH)
 
     def all_reduce(bufs, sems):
-        wg, w_swap, w_sum, w_in, w_part, z_in, w_done, z_all, w_row, w_all = bufs
-        swap_sems, in_sems, z_sems, back_sems, out_sems = [sems[2 * i : 2 * i + 2] for i in range(5)]
+        wg, w_swap, w_sum, w_in, w_part, z_all, w_row, w_all = bufs
+        swap_sems, in_sems, z_sems, out_sems = [sems[2 * i : 2 * i + 2] for i in range(4)]
         swap = [
             send(wg.at[1 - core], w_swap, swap_sems, 0, partner),
             send(w_all.at[core], w_all.at[core], swap_sems, 1, partner),
@@ -200,10 +205,7 @@
             return send(w_sum.at[lax.rem(scan + d, PLANE)], w_in.at[d - 1], in_sems, d - 1, plane[d - 1])
 
         def in_column(d):
-            return send(w_part.at[to_offset(d)], z_in.at[d - 1], z_sems, d - 1, on_chip(d, core))
-
-        def back_column(d):
-            return send(w_done, z_all.at[chip], back_sems, d - 1, on_chip(d, core))
+            return send(w_part, z_all.at[chip], z_sems, d - 1, on_chip(d, core))
 
         def back_plane(d):
             return send(w_row, w_all.at[core, scan], out_sems, d - 1, plane[d - 1])
@@ -220,32 +222,25 @@
             total = w_sum[scan].astype(F32)
             for d in range(PLANE - 1):
                 total = total + w_in[d].astype(F32)
-            for c in range(CHIPS):
-                w_part[c] = total[c * PIECE : (c + 1) * PIECE, :]
+            part = total.astype(BF16)
+            w_part[...] = part
+            z_all[chip] = part
             for d in range(1, CHIPS):
                 in_column(d).start()
 
         def stage_3():
             for d in range(1, CHIPS):
                 in_column(d).wait_recv()
-            total = w_part[chip]
-            for d in range(CHIPS - 1):
-                total = total + z_in[d]
-            w_done[...] = total
-            z_all[chip] = total
-            for d in range(1, CHIPS):
-                back_column(d).start()
-
-        def stage_4():
-            for d in range(1, CHIPS):
-                back_column(d).wait_recv()
-            row = jnp.concatenate([z_all[c] for c in range(CHIPS)], axis=0).astype(BF16)
+            total = z_all[0].astype(F32)
+            for c in range(1, CHIPS):
+                total = total + z_all[c].astype(F32)
+            row = total.astype(BF16)
             w_row[...] = row
             w_all[core, scan] = row
             for d in range(1, PLANE):
                 back_plane(d).start()
 
-        def stage_5():
+        def stage_4():
             for d in range(1, PLANE):
                 back_plane(d).wait_recv()
             swap[1].start()
@@ -253,11 +248,11 @@
         def left():
             for copy in swap:
                 copy.wait_send()
-            for make, count in ((in_plane, PLANE), (in_column, CHIPS), (back_column, CHIPS), (back_plane, PLANE)):
+            for make, count in ((in_plane, PLANE), (in_column, CHIPS), (back_plane, PLANE)):
                 for d in range(1, count):
                     make(d).wait_send()
 
-        return swap[0].start, stage_1, stage_2, stage_3, stage_4, stage_5, swap[1].wait_recv, left
+        return swap[0].start, stage_1, stage_2, stage_3, stage_4, swap[1].wait_recv, left
 
     q_rows = nn(ref[...], wq[...]).astype(BF16)
     for head in range(HEADS):
@@ -281,6 +276,7 @@
         part = ga_rows[:, group_cols(head)]
         gam[head] = jnp.where(own_lanes(ROWS, head), part, jnp.zeros_like(part))
     wvt = wv[...].T
+    wkt = wk[...].T
     own.wait()
 
     def near_first(step):
@@ -318,7 +314,7 @@
         send(src, src_all.at[tile * 2 + 1 - core], (sa1, ra1), d, partner).wait_recv()
         rows = src_all[pl.ds(tile * 2, 2)].reshape(TILE, D)
         k_tile = nn(rows, wk[...]).astype(BF16)
-        k_scr[tile] = k_tile
+        kt_scr[tile] = nt(wkt, rows).astype(BF16)
         v_scr[tile] = nn(rows, wv[...]).astype(BF16)
         vt_scr[tile] = nt(wvt, rows).astype(BF16)
         for head in range(HEADS):
@@ -367,15 +363,21 @@
     def _(tile):
         collect_columns(tile, log_sum, lc_chip, lc_in, lc_all, (sl1, rl1))
         rows = src_all[pl.ds(tile * 2, 2)].reshape(TILE, D)
-        for head in range(HEADS):
+
+        def make_match(head):
             lc_row = jnp.concatenate([lc_all[tile, kb, head : head + 1, :] for kb in range(2)], axis=1)
-            match = jnp.exp2(nt(qf[head], kh[tile, head]) * UNIT - lc_row).astype(BF16)
-            att[head] += by_halves(match, v_scr[tile, :, group_cols(head)])
+            match_scr[head] = jnp.exp2(nt(qf[head], kh[tile, head]) * UNIT - lc_row).astype(BF16)
+
+        def use_match(head):
+            match = match_scr[head]
+            att[head] += nt(vt_scr[tile, head_lanes(head), :], match)
             gvt = nn(gat_scr[head_lanes(head), :], match)
             gvt_scr[tile, head_lanes(head), :] = gvt.astype(BF16)
             dots = (gvt * vt_scr[tile, head_lanes(head), :].astype(F32)).sum(axis=0, keepdims=True)
             for kb in range(2):
                 cd_part[tile, kb, head : head + 1, :] = dots[:, kb * BLOCK : (kb + 1) * BLOCK]
+
+        in_turn(make_match, use_match)
         swap_columns(tile, cd_part, cd_swap, (sc0, rc0)).start()
         wvg[...] += nn(gvt_scr[tile], rows)
 
@@ -385,18 +387,14 @@
 
     spread_columns(TILES - 1, plain_sum, cd_part, cd_swap, cd_chip, cd_in, (sc0, rc0), (sc1, rc1))
 
+    att_t = att[...].reshape(D, ROWS)
+    att_rows = att_t.T
     for head in range(HEADS):
-        mask = own_lanes(ROWS, head)
-        value = jnp.where(mask, att[head], 0.0)
-        rd = (value * gam[head].astype(F32)).sum(axis=1, keepdims=True)
+        rd = (att_rows[:, group_cols(head)] * gam[head].astype(F32)).sum(axis=1, keepdims=True)
         rd_scr[head] = jnp.broadcast_to(rd, (ROWS, BLOCK))
-        if head % 2 == 0:
-            att_all[:, group_cols(head)] = value.astype(BF16)
-        else:
-            att_all[:, group_cols(head)] = jnp.where(mask, value.astype(BF16), att_all[:, group_cols(head)])
         gam[head] = gam[head] + gam[head]
-    matched_out[...] = (ref[...].astype(F32) + nn(att_all[...], wo[...])).astype(BF16)
-    pack_weight(early_bufs[0], 1, nn(att_all[...].T, gout[...]))
+    out[:ROWS] = (ref[...].astype(F32) + nn(att_rows.astype(BF16), wo[...])).astype(BF16)
+    pack_weight(early_bufs[0], 1, nn(att_t.astype(BF16), gout[...]))
     pack_weight(early_bufs[0], 0, wvg[...].T)
     early = all_reduce(early_bufs, early_sems)
     early[0]()
@@ -418,7 +416,7 @@
     @pl.loop(0, TILES)
     def _(step):
         tile = by_quarters(step)
-        for at, stage in ((1, 1), (3, 2), (6, 3)):
+        for at, stage in ((1, 1), (5, 2)):
 
             @pl.when(step == at)
             def _():
@@ -427,7 +425,8 @@
         collect_columns(tile, plain_sum, cd_chip, cd_in, cd_all, (sc1, rc1))
         rows = src_all[pl.ds(tile * 2, 2)].reshape(TILE, D)
         gk_heads = []
-        for head in range(HEADS):
+
+        def make_grad(head):
             cols = group_cols(head)
             x = nt(qb_scr[head], kh[tile, head])
             gp = nt(gam[head], v_scr[tile, :, cols])
@@ -439,11 +438,14 @@
                 u = x[:, lanes] * UNIT
                 r = jnp.exp2(u)
                 c = jnp.exp2(u + lr[head] - lc_row)
-                match = (r * c).astype(BF16).astype(F32)
-                lines.append((match * gp[:, lanes] - r * rd_scr[head] - c * cd_row).astype(BF16))
-            gs = jnp.concatenate(lines, axis=1)
-            gq[head] += by_halves(gs, k_scr[tile, :, cols])
+                lines.append((r * (c * gp[:, lanes] - rd_scr[head]) - c * cd_row).astype(BF16))
+            match_scr[head] = jnp.concatenate(lines, axis=1)
+
+        def use_grad(head):
+            gs = match_scr[head]
+            gq[head] += nt(kt_scr[tile, head_lanes(head), :], gs)
             gk_heads.append((nn(qt_all[head_lanes(head), :], gs) * SCALE).astype(BF16))
+        in_turn(make_grad, use_grad)
         gkt = jnp.concatenate(gk_heads, axis=0)
         wkg[...] += nn(gkt, rows)
         gst = nn(wk[...], gkt) + nn(wv[...], gvt_scr[tile])
@@ -455,39 +457,33 @@
         def _():
             spread_source(by_quarters(step - 1))
 
-    for head in range(HEADS):
-        mask = own_lanes(ROWS, head)
-        value = (gq[head] * SCALE).astype(BF16)
-        if head % 2 == 0:
-            gq_all[:, group_cols(head)] = value
-        else:
-            gq_all[:, group_cols(head)] = jnp.where(mask, value, gq_all[:, group_cols(head)])
-    pack_weight(late_bufs[0], 0, nn(ref[...].T, gq_all[...]))
+    gq_t = (gq[...].reshape(D, ROWS) * SCALE).astype(BF16)
+    pack_weight(late_bufs[0], 0, nn(gq_t, ref[...]).T)
     pack_weight(late_bufs[0], 1, wkg[...].T)
     late = all_reduce(late_bufs, late_sems)
     late[0]()
+    early[3]()
+    gref = (gout[...].astype(F32) + nt(gq_t.T, wq[...])).astype(BF16)
+    late[1]()
+    out[ROWS : 2 * ROWS] = gref
+    spread_source(by_quarters(TILES - 1))
     early[4]()
-    gref_out[...] = (gout[...].astype(F32) + nt(gq_all[...], wq[...])).astype(BF16)
-    late[1]()
-    spread_source(by_quarters(TILES - 1))
-    early[5]()
     late[2]()
-    late[3]()
     for d in (4, 3, 5, 2, 6, 1, 7):
         source_copy(d).wait_recv()
     gsrc = gs_sum[chip].astype(F32)
     for d in range(CHIPS - 1):
         gsrc = gsrc + gs_in[d].astype(F32)
-    gsrc_out[...] = gsrc.T.astype(BF16)
-    early[6]()
-    early_out[...] = early_bufs[-1][...]
+    out[2 * ROWS : 2 * ROWS + BLOCK] = gsrc.T.astype(BF16)
+    early[5]()
+    put_weights(out, early_bufs[-1], 1)
+    late[3]()
     late[4]()
     late[5]()
+    put_weights(out, late_bufs[-1], 0)
+
+    early[6]()
     late[6]()
-    late_out[...] = late_bufs[-1][...]
-
-    early[7]()
-    late[7]()
     for way in range(2):
         for hops in range(1, 5):
             for piece in pieces_of(way, hops):
@@ -516,59 +512,57 @@
     row = (CHUNK, BLOCK)
     reduction = [
         vm((2, PLANE) + row, BF16), vm((PLANE,) + row, BF16), vm((PLANE,) + row, BF16), vm((PLANE - 1,) + row, BF16),
-        vm((CHIPS, PIECE, BLOCK), F32), vm((CHIPS - 1, PIECE, BLOCK), F32), vm((PIECE, BLOCK), F32),
-        vm((CHIPS, PIECE, BLOCK), F32), vm(row, BF16), vm((2, PLANE) + row, BF16),
+        vm(row, BF16), vm((CHIPS,) + row, BF16), vm(row, BF16), vm((2, PLANE) + row, BF16),
     ]
     heads = (HEADS, ROWS, BLOCK)
+    turned = (HEADS, HEAD_DIM, ROWS)
     pair = (TILES, 2, HEADS, BLOCK)
     columns = [vm(pair, F32), vm(pair, F32), vm(pair, F32), vm((TILES, CHIPS - 1, 2, HEADS, BLOCK), F32), vm(pair, F32)]
     scratch = [
-        vm((2 * CHIPS, BLOCK, D), BF16), vm((TILES, TILE, D), BF16), vm((TILES, HEADS, TILE, BLOCK), BF16),
+        vm((2 * CHIPS, BLOCK, D), BF16), vm((TILES, D, TILE), BF16), vm((TILES, HEADS, TILE, BLOCK), BF16),
         vm((TILES, TILE, D), BF16), vm((TILES, D, TILE), BF16), vm(heads, BF16), vm(heads, BF16), vm(heads, BF16),
         vm(heads, BF16), vm((D, ROWS), BF16), vm((D, ROWS), BF16), vm((TILES, HEADS, ROWS, TILE), F32), vm(heads, F32), vm(heads, F32),
         *columns, *columns,
-        vm(heads, F32), vm((ROWS, D), BF16), vm((TILES, D, TILE), BF16), vm(heads, F32), vm((D, D), F32),
-        vm((D, D), F32), vm(heads, F32), vm((ROWS, D), BF16),
+        vm(turned, F32), vm((HEADS, ROWS, TILE), BF16), vm((TILES, D, TILE), BF16), vm(heads, F32), vm((D, D), F32), vm((D, D), F32), vm(turned, F32),
         vm((TILES, 2, D, BLOCK), BF16), vm((TILES, D, BLOCK), BF16), vm((TILES, D, BLOCK), BF16),
         vm((CHIPS - 1, D, BLOCK), BF16),
         *reduction, *reduction,
         DMA, DMA((16,)), DMA((16,)),
-    ] + [DMA((n,)) for n in (8,) * 14 + 2 * (2, 2, 15, 15, 7, 7, 7, 7, 15, 15)]
+    ] + [DMA((n,)) for n in (8,) * 14 + 2 * (2, 2, 15, 15, 7, 7, 15, 15)]
     return pl.pallas_call(
         layer_kernel,
-        out_shape=[shape((ROWS, D), BF16)] * 2 + [shape((BLOCK, D), BF16)] + [shape((2, PLANE) + row, BF16)] * 2,
+        out_shape=shape((OUT_ROWS, D), BF16),
         in_specs=[VMEM] * 7 + [SMEM],
-        out_specs=[VMEM] * 5,
+        out_specs=VMEM,
         scratch_shapes=scratch,
         compiler_params=pltpu.CompilerParams(vmem_limit_bytes=60 << 20, collective_id=1, has_side_effects=True),
         name="layer",
     )(ref, gout, src, wq, wk, wv, wo, inter)
 
 
-def finish_kernel(matched, gref, gsrc, early, late, matched_out, gref_out, gsrc_out, wq_out, wk_out, wv_out, wo_out):
-    matched_out[...] = matched[...]
-    gref_out[...] = gref[...]
-    gsrc_out[...] = gsrc[...]
-    unpack_weight(wq_out, late, 0)
-    unpack_weight(wk_out, late, 1)
-    unpack_weight(wv_out, early, 0)
-    unpack_weight(wo_out, early, 1)
-
-
-def finish(*parts):
+def finish_kernel(parts, matched_out, gref_out, gsrc_out, *weights):
+    matched_out[...] = parts[:ROWS]
+    gref_out[...] = parts[ROWS : 2 * ROWS]
+    gsrc_out[...] = parts[2 * ROWS : 2 * ROWS + BLOCK]
+    for at, out in enumerate(weights):
+        first = 2 * ROWS + BLOCK + at * D
+        out[...] = parts[first : first + D].astype(F32)
+
+
+def finish(parts):
     return pl.pallas_call(
         finish_kernel,
         out_shape=[shape((ROWS, D), BF16)] * 2 + [shape((BLOCK, D), BF16)] + [shape((D, D), F32)] * 4,
-        in_specs=[VMEM] * 5,
+        in_specs=[VMEM],
         out_specs=[VMEM] * 7,
         compiler_params=pltpu.CompilerParams(vmem_limit_bytes=32 << 20),
         name="finish",
-    )(*parts)
+    )(parts)
 
 
 def on_device(ref_feats, src_feats, grad_out, w_query, w_key, w_value, w_out, intersection):
     parts = layer(ref_feats[0], grad_out[0], src_feats[0], w_query, w_key, w_value, w_out, intersection[0])
-    matched, gref, gsrc, wqg, wkg, wvg, wog = finish(*parts)
+    matched, gref, gsrc, wqg, wkg, wvg, wog = finish(parts)
     return matched[None], gref[None], gsrc[None], wqg, wkg, wvg, wog
 
 

time: 101 us -> 86.7 us (0.86)
  Pallas kernels: 95.7 us -> 84.7 us
  local copies, waits for them, and re-layouts: 4.63 us -> 1.24 us
    pallas_call x1, Pallas kernels: 94.4 us -> 83.5 us  [layer(): pl.pallas_call(layer_kernel, out_shape=shape((OUT_ROWS, D), BF16), in_spe...]
    unnamed x10 -> x2, local copies, waits for them, and re-layouts: 4.63 us -> 1.24 us
where the time goes in v4:
time: 86.7 us; the launch traced here: 86.6 us
  Pallas kernels  84.7 us (98%)
  local copies, waits for them, and re-layouts  1.24 us (1%)
    pallas_call x1, Pallas kernels, layer(): pl.pallas_call(layer_kernel, out_shape=shape((OUT_ROWS, D), BF16), in_spe...  83.5 us

profile of v4, /device:TPU:1, one launch (start us, length us, event | category | flops | bytes accessed | tf_op | source)
XLA Modules:
  0.0 86.6 jit_solution(5142940283150629717)
XLA Ops:
  0.6 83.5 %layer.1.parts = bf16[2176,256]{1,0:T(8,128)(2,1)} custom-call(bf16[512,256]{1,0:T(8,128)(2,1)} %bitcast.7, bf16[512,256]{1,0:T(8,128)(2,1)} %bitcast.8, bf16[128,256]{1,0:T(8,128)(2,1)} %bitcast.9, bf16[256,256]{1,0:T(8,128)(2,1)} %wq.1, bf16[256,256]{1,0:T(8,128)(2,1)} %wk.1, bf16[256,256]{1,0:T(8,128)(2,1)} %wv.1, bf16[256,256]{1,0:T(8,128)(2,1)} %wo.1, ...), custom_call_target="tpu_custom_call" | custom-call | tf_op jit(solution)/shard_map/layer/pallas_call | solution.py:532
  84.1 0.0 copy-start
  84.1 1.2 %copy-done = bf16[2176,256]{1,0:T(8,128)(2,1)S(1)} copy-done((bf16[2176,256]{1,0:T(8,128)(2,1)S(1)}, bf16[2176,256]{1,0:T(8,128)(2,1)}, u32[]{:S(2)}) %copy-start) | copy-done | bytes 1114136
  85.3 1.2 %finish.1 = (bf16[512,256]{1,0:T(8,128)(2,1)}, bf16[512,256]{1,0:T(8,128)(2,1)}, bf16[128,256]{1,0:T(8,128)(2,1)}, f32[256,256]{1,0:T(8,128)}, f32[256,256]{1,0:...) custom-call(bf16[2176,256]{1,0:T(8,128)(2,1)S(1)} %copy-done), custom_call_target="tpu_custom_call" | custom-call | tf_op jit(solution)/shard_map/finish/pallas_call | solution.py:553
Async XLA Ops:
  84.1 1.2 %copy-start = (bf16[2176,256]{1,0:T(8,128)(2,1)S(1)}, bf16[2176,256]{1,0:T(8,128)(2,1)}, u32[]{:S(2)}) copy-start(bf16[2176,256]{1,0:T(8,128)(2,1)} %layer.1.parts) | copy-start | bytes 3342340

commit v5 on v4

--- a/solution.py
+++ b/solution.py
@@ -21,6 +21,7 @@
 CHIPS = 8
 PLANE = 16
 CHUNK = 32
+PIECES = 4
 OUT_ROWS = 2 * ROWS + BLOCK + 4 * D
 NEG = -1.0e30
 SCALE = HEAD_DIM**-0.5
@@ -29,6 +30,7 @@
 BF16 = jnp.bfloat16
 MESH = pl.DeviceIdType.MESH
 VMEM = pl.BlockSpec(memory_space=pltpu.VMEM)
+HBM = pl.BlockSpec(memory_space=pltpu.HBM)
 SMEM = pl.BlockSpec(memory_space=pltpu.SMEM)
 DMA = pltpu.SemaphoreType.DMA
 
@@ -140,15 +142,15 @@
 
 def layer_kernel(
     ref, gout, src, wq, wk, wv, wo, inter,
-    out,
-    src_all, kt_scr, kh, v_scr, vt_scr, qs, qf, qb_scr, gam, gat_scr, qt_all, t_scr, rm, lr,
+    out_hbm,
+    out, src_all, kt_scr, kh, v_scr, vt_scr, qs, qf, qb_scr, gam, gat_scr, qt_all, t_scr, rm, lr,
     lc_part, lc_swap, lc_chip, lc_in, lc_all, cd_part, cd_swap, cd_chip, cd_in, cd_all,
     att, match_scr, gvt_scr, rd_scr, wvg, wkg, gq,
     gs_part, gs_swap, gs_sum, gs_in, *rest,
 ):
     early_bufs, late_bufs, rest = rest[:8], rest[8:16], rest[16:]
     own_sem, sa0, ra0, sa1, ra1, sl0, rl0, sl1, rl1, sc0, rc0, sc1, rc1, sg0, rg0, sg1, rg1 = rest[:17]
-    early_sems, late_sems = rest[17:25], rest[25:33]
+    early_sems, late_sems, out_sems = rest[17:25], rest[25:33], rest[33]
     blk = lax.axis_index("blk")
     scan = lax.axis_index("scan")
     chip = lax.div(blk, 2)
@@ -165,20 +167,22 @@
         return lax.rem(chip + d, CHIPS)
 
     def ring_copy(block, way, hops, piece, source=None):
-        rows = pl.ds(piece * (BLOCK // 2), BLOCK // 2)
+        rows = pl.ds(piece * (BLOCK // PIECES), BLOCK // PIECES)
         landing = src_all.at[block, rows]
         return send(
             landing if source is None else source.at[rows], landing, (sa0, ra0),
-            way * 8 + (hops - 1) * 2 + piece, on_chip(1 if way == 0 else CHIPS - 1, core),
+            (way * 4 + hops - 1) * PIECES + piece, on_chip(1 if way == 0 else CHIPS - 1, core),
         )
 
     def pieces_of(way, hops):
-        return range(2) if hops < 4 else (way,)
+        return range(PIECES) if hops < 4 else range(way * PIECES // 2, (way + 1) * PIECES // 2)
 
     def relay(hops):
-        for way in range(2):
-            origin = from_offset(hops if way == 0 else CHIPS - hops) * 2 + core
-            for piece in pieces_of(way, hops):
+        for piece in range(PIECES):
+            for way in range(2):
+                if piece not in pieces_of(way, hops):
+                    continue
+                origin = from_offset(hops if way == 0 else CHIPS - hops) * 2 + core
                 ring_copy(origin, way, hops, piece).wait_recv()
                 if hops < 4 and piece in pieces_of(way, hops + 1):
                     ring_copy(origin, way, hops + 1, piece).start()
@@ -265,7 +269,7 @@
     own.start()
 
     pl.semaphore_wait(barrier, len(everyone))
-    for piece in range(2):
+    for piece in range(PIECES):
         for way in range(2):
             ring_copy(blk, way, 1, piece, src).start()
     send(src, src_all.at[blk], (sa1, ra1), 0, partner).start()
@@ -461,6 +465,11 @@
     pack_weight(late_bufs[0], 0, nn(gq_t, ref[...]).T)
     pack_weight(late_bufs[0], 1, wkg[...].T)
     late = all_reduce(late_bufs, late_sems)
+
+    def leave(at, first, count):
+        rows = pl.ds(first, count)
+        return pltpu.make_async_copy(out.at[rows], out_hbm.at[rows], out_sems.at[at])
+
     late[0]()
     early[3]()
     gref = (gout[...].astype(F32) + nt(gq_t.T, wq[...])).astype(BF16)
@@ -475,15 +484,13 @@
     for d in range(CHIPS - 1):
         gsrc = gsrc + gs_in[d].astype(F32)
     out[2 * ROWS : 2 * ROWS + BLOCK] = gsrc.T.astype(BF16)
+    leave(0, 0, 2 * ROWS + BLOCK).start()
     early[5]()
     put_weights(out, early_bufs[-1], 1)
+    leave(1, OUT_ROWS - 2 * D, 2 * D).start()
     late[3]()
-    late[4]()
-    late[5]()
-    put_weights(out, late_bufs[-1], 0)
 
     early[6]()
-    late[6]()
     for way in range(2):
         for hops in range(1, 5):
             for piece in pieces_of(way, hops):
@@ -501,6 +508,16 @@
         @pl.when(tile > 0)
         def _():
             send(gs_sum.at[tile], gs_in.at[0], (sg1, rg1), tile, partner).wait_send()
+
+    late[4]()
+    late[5]()
+    put_weights(out, late_bufs[-1], 0)
+    leave(2, 2 * ROWS + BLOCK, 2 * D).start()
+    leave(2, 2 * ROWS + BLOCK, 2 * D).wait()
+    leave(1, OUT_ROWS - 2 * D, 2 * D).wait()
+    leave(0, 0, 2 * ROWS + BLOCK).wait()
+
+    late[6]()
 
 
 def shape(dims, dtype):
@@ -519,6 +536,7 @@
     pair = (TILES, 2, HEADS, BLOCK)
     columns = [vm(pair, F32), vm(pair, F32), vm(pair, F32), vm((TILES, CHIPS - 1, 2, HEADS, BLOCK), F32), vm(pair, F32)]
     scratch = [
+        vm((OUT_ROWS, D), BF16),
         vm((2 * CHIPS, BLOCK, D), BF16), vm((TILES, D, TILE), BF16), vm((TILES, HEADS, TILE, BLOCK), BF16),
         vm((TILES, TILE, D), BF16), vm((TILES, D, TILE), BF16), vm(heads, BF16), vm(heads, BF16), vm(heads, BF16),
         vm(heads, BF16), vm((D, ROWS), BF16), vm((D, ROWS), BF16), vm((TILES, HEADS, ROWS, TILE), F32), vm(heads, F32), vm(heads, F32),
@@ -527,35 +545,53 @@
         vm((TILES, 2, D, BLOCK), BF16), vm((TILES, D, BLOCK), BF16), vm((TILES, D, BLOCK), BF16),
         vm((CHIPS - 1, D, BLOCK), BF16),
         *reduction, *reduction,
-        DMA, DMA((16,)), DMA((16,)),
-    ] + [DMA((n,)) for n in (8,) * 14 + 2 * (2, 2, 15, 15, 7, 7, 15, 15)]
+        DMA, DMA((8 * PIECES,)), DMA((8 * PIECES,)),
+    ] + [DMA((n,)) for n in (8,) * 14 + 2 * (2, 2, 15, 15, 7, 7, 15, 15) + (3,)]
     return pl.pallas_call(
         layer_kernel,
         out_shape=shape((OUT_ROWS, D), BF16),
         in_specs=[VMEM] * 7 + [SMEM],
-        out_specs=VMEM,
+        out_specs=HBM,
         scratch_shapes=scratch,
         compiler_params=pltpu.CompilerParams(vmem_limit_bytes=60 << 20, collective_id=1, has_side_effects=True),
         name="layer",
     )(ref, gout, src, wq, wk, wv, wo, inter)
 
 
-def finish_kernel(parts, matched_out, gref_out, gsrc_out, *weights):
-    matched_out[...] = parts[:ROWS]
-    gref_out[...] = parts[ROWS : 2 * ROWS]
-    gsrc_out[...] = parts[2 * ROWS : 2 * ROWS + BLOCK]
+def finish_kernel(parts, matched_out, gref_out, gsrc_out, *rest):
+    weights, (rows, packed, wide, in_sems, out_sems) = rest[:4], rest[4:]
+    first = 2 * ROWS + BLOCK
+    load_weights = pltpu.make_async_copy(parts.at[pl.ds(first, 4 * D)], packed, in_sems.at[0])
+    load_rows = pltpu.make_async_copy(parts.at[pl.ds(0, first)], rows, in_sems.at[1])
+    load_weights.start()
+    load_rows.start()
+    stores = []
+    load_weights.wait()
     for at, out in enumerate(weights):
-        first = 2 * ROWS + BLOCK + at * D
-        out[...] = parts[first : first + D].astype(F32)
+        wide[at] = packed[at * D : (at + 1) * D].astype(F32)
+        stores.append(pltpu.make_async_copy(wide.at[at], out, out_sems.at[at]))
+        stores[-1].start()
+    load_rows.wait()
+    for at, (out, begin, count) in enumerate(
+        ((matched_out, 0, ROWS), (gref_out, ROWS, ROWS), (gsrc_out, 2 * ROWS, BLOCK))
+    ):
+        stores.append(pltpu.make_async_copy(rows.at[pl.ds(begin, count)], out, out_sems.at[4 + at]))
+        stores[-1].start()
+    for store in stores:
+        store.wait()
 
 
 def finish(parts):
     return pl.pallas_call(
         finish_kernel,
         out_shape=[shape((ROWS, D), BF16)] * 2 + [shape((BLOCK, D), BF16)] + [shape((D, D), F32)] * 4,
-        in_specs=[VMEM],
-        out_specs=[VMEM] * 7,
-        compiler_params=pltpu.CompilerParams(vmem_limit_bytes=32 << 20),
+        in_specs=[HBM],
+        out_specs=[HBM] * 7,
+        scratch_shapes=[
+            pltpu.VMEM((2 * ROWS + BLOCK, D), BF16), pltpu.VMEM((4 * D, D), BF16), pltpu.VMEM((4, D, D), F32),
+            DMA((2,)), DMA((7,)),
+        ],
+        compiler_params=pltpu.CompilerParams(vmem_limit_bytes=60 << 20),
         name="finish",
     )(parts)
 

time: 86.7 us -> 86 us (level)
  local copies, waits for them, and re-layouts: 1.24 us -> 0 us
    unnamed x2 -> x0, local copies, waits for them, and re-layouts: 1.24 us -> none
    pallas_call x1, Pallas kernels: 1.25 us -> 2.28 us  [finish(): pl.pallas_call(finish_kernel, out_shape=[shape((ROWS, D), BF16)] * 2 + [s...]
where the time goes in v5:
time: 86 us; the launch traced here: 85.8 us
  Pallas kernels  85.2 us (99%)
    pallas_call x1, Pallas kernels, layer(): pl.pallas_call(layer_kernel, out_shape=shape((OUT_ROWS, D), BF16), in_spe...  82.9 us
    pallas_call x1, Pallas kernels, finish(): pl.pallas_call(finish_kernel, out_shape=[shape((ROWS, D), BF16)] * 2 + [s...  2.28 us

profile of v5, /device:TPU:1, one launch (start us, length us, event | category | flops | bytes accessed | tf_op | source)
XLA Modules:
  0.0 85.8 jit_solution(4903256405740766849)
XLA Ops:
  0.6 82.9 %layer.1.parts = bf16[2176,256]{1,0:T(8,128)(2,1)} custom-call(bf16[512,256]{1,0:T(8,128)(2,1)} %bitcast.7, bf16[512,256]{1,0:T(8,128)(2,1)} %bitcast.8, bf16[128,256]{1,0:T(8,128)(2,1)} %bitcast.9, bf16[256,256]{1,0:T(8,128)(2,1)} %wq.1, bf16[256,256]{1,0:T(8,128)(2,1)} %wk.1, bf16[256,256]{1,0:T(8,128)(2,1)} %wv.1, bf16[256,256]{1,0:T(8,128)(2,1)} %wo.1, ...), custom_call_target="tpu_custom_call" | custom-call | tf_op jit(solution)/shard_map/layer/pallas_call | solution.py:550
  83.6 2.3 %finish.1 = (bf16[512,256]{1,0:T(8,128)(2,1)}, bf16[512,256]{1,0:T(8,128)(2,1)}, bf16[128,256]{1,0:T(8,128)(2,1)}, f32[256,256]{1,0:T(8,128)}, f32[256,256]{1,0:...) custom-call(bf16[2176,256]{1,0:T(8,128)(2,1)} %layer.1.parts), custom_call_target="tpu_custom_call" | custom-call | tf_op jit(solution)/shard_map/finish/pallas_call | solution.py:585

commit v6 on v5

--- a/solution.py
+++ b/solution.py
@@ -150,7 +150,7 @@
 ):
     early_bufs, late_bufs, rest = rest[:8], rest[8:16], rest[16:]
     own_sem, sa0, ra0, sa1, ra1, sl0, rl0, sl1, rl1, sc0, rc0, sc1, rc1, sg0, rg0, sg1, rg1 = rest[:17]
-    early_sems, late_sems, out_sems = rest[17:25], rest[25:33], rest[33]
+    early_sems, late_sems, out_sems, known = rest[17:25], rest[25:33], rest[33], rest[34]
     blk = lax.axis_index("blk")
     scan = lax.axis_index("scan")
     chip = lax.div(blk, 2)
@@ -191,9 +191,20 @@
             send(src_all.at[origin], src_all.at[origin], (sa1, ra1), d, partner).start()
 
     plane = [{"scan": lax.rem(scan + d, PLANE)} for d in range(1, PLANE)]
-    column = [on_chip(d, c) for d in range(1, CHIPS) for c in range(2)]
     barrier = pltpu.get_barrier_semaphore()
-    everyone = [partner] + column + plane
+    row_at, col_at = lax.div(scan, 4), lax.rem(scan, 4)
+    beside_z = [on_chip(1, core), on_chip(CHIPS - 1, core)]
+    beside_x = [{"scan": row_at * 4 + lax.rem(col_at + d, 4)} for d in (1, 3)]
+    beside_y = [{"scan": lax.rem(row_at + d, 4) * 4 + col_at} for d in (1, 3)]
+    everyone = [partner] + beside_z + beside_x + beside_y
+
+    def tell(at, targets):
+        for target in targets:
+            pl.semaphore_signal(known.at[at], inc=1, device_id=target, device_id_type=MESH)
+
+    def hear(at):
+        pl.semaphore_wait(known.at[at], 2)
+
     for target in everyone:
         pl.semaphore_signal(barrier, inc=1, device_id=target, device_id_type=MESH)
 
@@ -273,6 +284,8 @@
         for way in range(2):
             ring_copy(blk, way, 1, piece, src).start()
     send(src, src_all.at[blk], (sa1, ra1), 0, partner).start()
+    tell(0, beside_z)
+    tell(4, beside_x)
 
     ga_rows = nt(gout[...], wo[...]).astype(BF16)
     gat_scr[...] = nt(wo[...], gout[...]).astype(BF16)
@@ -282,6 +295,8 @@
     wvt = wv[...].T
     wkt = wk[...].T
     own.wait()
+    hear(0)
+    tell(1, beside_z)
 
     def near_first(step):
         half = lax.div(step + 1, 2)
@@ -308,6 +323,25 @@
     def _(step):
         d = near_first(step)
         tile = from_offset(d)
+
+        @pl.when(step == 1)
+        def _():
+            hear(2)
+            tell(3, beside_z)
+
+        @pl.when(step == 2)
+        def _():
+            hear(4)
+            tell(5, beside_y)
+
+        @pl.when(step == 4)
+        def _():
+            hear(5)
+            tell(6, beside_y)
+
+        @pl.when(step == 6)
+        def _():
+            hear(6)
 
         for at, hops in ((1, 1), (2, 2), (4, 3), (6, 4)):
 
@@ -334,6 +368,15 @@
                 lc_part[tile, kb, head : head + 1, :] = lse[:, kb * BLOCK : (kb + 1) * BLOCK]
         swap_columns(tile, lc_part, lc_swap, (sl0, rl0)).start()
 
+        @pl.when(step == 0)
+        def _():
+            hear(1)
+            tell(2, beside_z)
+
+        @pl.when(step == 1)
+        def _():
+            hear(3)
+
         @pl.when(step > 0)
         def _():
             before = from_offset(near_first(step - 1))
@@ -432,18 +475,20 @@
 
         def make_grad(head):
             cols = group_cols(head)
-            x = nt(qb_scr[head], kh[tile, head])
-            gp = nt(gam[head], v_scr[tile, :, cols])
-            lines = []
-            for kb in range(2):
-                lanes = slice(kb * BLOCK, (kb + 1) * BLOCK)
-                lc_row = lc_all[tile, kb, head : head + 1, :]
-                cd_row = cd_all[tile, kb, head : head + 1, :]
-                u = x[:, lanes] * UNIT
-                r = jnp.exp2(u)
-                c = jnp.exp2(u + lr[head] - lc_row)
-                lines.append((r * (c * gp[:, lanes] - rd_scr[head]) - c * cd_row).astype(BF16))
-            match_scr[head] = jnp.concatenate(lines, axis=1)
+            for half in range(2):
+                rows = slice(half * TILE, (half + 1) * TILE)
+                x = nt(qb_scr[head, rows], kh[tile, head])
+                gp = nt(gam[head, rows], v_scr[tile, :, cols])
+                lines = []
+                for kb in range(2):
+                    lanes = slice(kb * BLOCK, (kb + 1) * BLOCK)
+                    lc_row = lc_all[tile, kb, head : head + 1, :]
+                    cd_row = cd_all[tile, kb, head : head + 1, :]
+                    u = x[:, lanes] * UNIT
+                    r = jnp.exp2(u)
+                    c = jnp.exp2(u + lr[head, rows] - lc_row)
+                    lines.append((r * (c * gp[:, lanes] - rd_scr[head, rows]) - c * cd_row).astype(BF16))
+                match_scr[head, rows] = jnp.concatenate(lines, axis=1)
 
         def use_grad(head):
             gs = match_scr[head]
@@ -546,7 +591,7 @@
         vm((CHIPS - 1, D, BLOCK), BF16),
         *reduction, *reduction,
         DMA, DMA((8 * PIECES,)), DMA((8 * PIECES,)),
-    ] + [DMA((n,)) for n in (8,) * 14 + 2 * (2, 2, 15, 15, 7, 7, 15, 15) + (3,)]
+    ] + [DMA((n,)) for n in (8,) * 14 + 2 * (2, 2, 15, 15, 7, 7, 15, 15) + (3,)] + [pltpu.SemaphoreType.REGULAR((7,))]
     return pl.pallas_call(
         layer_kernel,
         out_shape=shape((OUT_ROWS, D), BF16),

time: 86 us -> 85.4 us (level)
  no operation moved by 1% of the time
where the time goes in v6:
time: 85.4 us; the launch traced here: 85.3 us
  Pallas kernels  84.7 us (99%)
    pallas_call x1, Pallas kernels, layer(): pl.pallas_call(layer_kernel, out_shape=shape((OUT_ROWS, D), BF16), in_spe...  82.4 us
    pallas_call x1, Pallas kernels, finish(): pl.pallas_call(finish_kernel, out_shape=[shape((ROWS, D), BF16)] * 2 + [s...  2.28 us

profile of v6, /device:TPU:1, one launch (start us, length us, event | category | flops | bytes accessed | tf_op | source)
XLA Modules:
  0.0 85.3 jit_solution(13489403024911073680)
XLA Ops:
  0.6 82.4 %layer.1.parts = bf16[2176,256]{1,0:T(8,128)(2,1)} custom-call(bf16[512,256]{1,0:T(8,128)(2,1)} %bitcast.7, bf16[512,256]{1,0:T(8,128)(2,1)} %bitcast.8, bf16[128,256]{1,0:T(8,128)(2,1)} %bitcast.9, bf16[256,256]{1,0:T(8,128)(2,1)} %wq.1, bf16[256,256]{1,0:T(8,128)(2,1)} %wk.1, bf16[256,256]{1,0:T(8,128)(2,1)} %wv.1, bf16[256,256]{1,0:T(8,128)(2,1)} %wo.1, ...), custom_call_target="tpu_custom_call" | custom-call | tf_op jit(solution)/shard_map/layer/pallas_call | solution.py:595
  83.0 2.3 %finish.1 = (bf16[512,256]{1,0:T(8,128)(2,1)}, bf16[512,256]{1,0:T(8,128)(2,1)}, bf16[128,256]{1,0:T(8,128)(2,1)}, f32[256,256]{1,0:T(8,128)}, f32[256,256]{1,0:...) custom-call(bf16[2176,256]{1,0:T(8,128)(2,1)} %layer.1.parts), custom_call_target="tpu_custom_call" | custom-call | tf_op jit(solution)/shard_map/finish/pallas_call | solution.py:630

commit v7 on v6

--- a/solution.py
+++ b/solution.py
@@ -295,8 +295,6 @@
     wvt = wv[...].T
     wkt = wk[...].T
     own.wait()
-    hear(0)
-    tell(1, beside_z)
 
     def near_first(step):
         half = lax.div(step + 1, 2)
@@ -324,30 +322,23 @@
         d = near_first(step)
         tile = from_offset(d)
 
-        @pl.when(step == 1)
-        def _():
-            hear(2)
-            tell(3, beside_z)
-
-        @pl.when(step == 2)
-        def _():
-            hear(4)
-            tell(5, beside_y)
-
-        @pl.when(step == 4)
-        def _():
-            hear(5)
-            tell(6, beside_y)
-
-        @pl.when(step == 6)
-        def _():
-            hear(6)
-
         for at, hops in ((1, 1), (2, 2), (4, 3), (6, 4)):
 
             @pl.when(step == at)
             def _():
                 relay(hops)
+
+        for at, rounds in (
+            (1, ((0, 1, beside_z),)), (2, ((1, 2, beside_z), (4, 5, beside_y))), (3, ((2, 3, beside_z),)),
+            (4, ((3, None, None), (5, 6, beside_y))), (6, ((6, None, None),)),
+        ):
+
+            @pl.when(step == at)
+            def _():
+                for heard, told, targets in rounds:
+                    hear(heard)
+                    if told is not None:
+                        tell(told, targets)
 
         send(src, src_all.at[tile * 2 + 1 - core], (sa1, ra1), d, partner).wait_recv()
         rows = src_all[pl.ds(tile * 2, 2)].reshape(TILE, D)
@@ -368,19 +359,19 @@
                 lc_part[tile, kb, head : head + 1, :] = lse[:, kb * BLOCK : (kb + 1) * BLOCK]
         swap_columns(tile, lc_part, lc_swap, (sl0, rl0)).start()
 
-        @pl.when(step == 0)
+        def spread(d):
+            spread_columns(
+                from_offset(d), log_sum, lc_part, lc_swap, lc_chip, lc_in, (sl0, rl0), (sl1, rl1)
+            )
+
+        @pl.when(step == 4)
         def _():
-            hear(1)
-            tell(2, beside_z)
-
-        @pl.when(step == 1)
+            for d in (0, 1, 7, 2):
+                spread(d)
+
+        @pl.when(step > 4)
         def _():
-            hear(3)
-
-        @pl.when(step > 0)
-        def _():
-            before = from_offset(near_first(step - 1))
-            spread_columns(before, log_sum, lc_part, lc_swap, lc_chip, lc_in, (sl0, rl0), (sl1, rl1))
+            spread(near_first(step - 1))
 
     spread_columns(
         from_offset(4), log_sum, lc_part, lc_swap, lc_chip, lc_in, (sl0, rl0), (sl1, rl1)

time: 85.4 us -> 84.6 us (level)
  Pallas kernels: 84.7 us -> 83.8 us
    pallas_call x1, Pallas kernels: 82.4 us -> 81.5 us  [layer(): pl.pallas_call(layer_kernel, out_shape=shape((OUT_ROWS, D), BF16), in_spe...]
where the time goes in v7:
time: 84.6 us; the launch traced here: 84.4 us
  Pallas kernels  83.8 us (99%)
    pallas_call x1, Pallas kernels, layer(): pl.pallas_call(layer_kernel, out_shape=shape((OUT_ROWS, D), BF16), in_spe...  81.5 us
    pallas_call x1, Pallas kernels, finish(): pl.pallas_call(finish_kernel, out_shape=[shape((ROWS, D), BF16)] * 2 + [s...  2.28 us

profile of v7, /device:TPU:1, one launch (start us, length us, event | category | flops | bytes accessed | tf_op | source)
XLA Modules:
  0.0 84.4 jit_solution(15303575635632023948)
XLA Ops:
  0.6 81.5 %layer.1.parts = bf16[2176,256]{1,0:T(8,128)(2,1)} custom-call(bf16[512,256]{1,0:T(8,128)(2,1)} %bitcast.7, bf16[512,256]{1,0:T(8,128)(2,1)} %bitcast.8, bf16[128,256]{1,0:T(8,128)(2,1)} %bitcast.9, bf16[256,256]{1,0:T(8,128)(2,1)} %wq.1, bf16[256,256]{1,0:T(8,128)(2,1)} %wk.1, bf16[256,256]{1,0:T(8,128)(2,1)} %wv.1, bf16[256,256]{1,0:T(8,128)(2,1)} %wo.1, ...), custom_call_target="tpu_custom_call" | custom-call | tf_op jit(solution)/shard_map/layer/pallas_call | solution.py:586
  82.2 2.3 %finish.1 = (bf16[512,256]{1,0:T(8,128)(2,1)}, bf16[512,256]{1,0:T(8,128)(2,1)}, bf16[128,256]{1,0:T(8,128)(2,1)}, f32[256,256]{1,0:T(8,128)}, f32[256,256]{1,0:...) custom-call(bf16[2176,256]{1,0:T(8,128)(2,1)} %layer.1.parts), custom_call_target="tpu_custom_call" | custom-call | tf_op jit(solution)/shard_map/finish/pallas_call | solution.py:621

commit v8 on v7

--- a/solution.py
+++ b/solution.py
@@ -141,16 +141,18 @@
 
 
 def layer_kernel(
-    ref, gout, src, wq, wk, wv, wo, inter,
+    ref_hbm, gout_hbm, src, wq_hbm, wk_hbm, wv_hbm, wo_hbm, inter,
     out_hbm,
-    out, src_all, kt_scr, kh, v_scr, vt_scr, qs, qf, qb_scr, gam, gat_scr, qt_all, t_scr, rm, lr,
+    ref, gout, wq, wk, wv, wo, out, src_all, kt_scr, kh, v_scr, vt_scr, qs, qf, qb_scr, gam, gat_scr, qt_all, t_scr, rm, lr,
     lc_part, lc_swap, lc_chip, lc_in, lc_all, cd_part, cd_swap, cd_chip, cd_in, cd_all,
     att, match_scr, gvt_scr, rd_scr, wvg, wkg, gq,
     gs_part, gs_swap, gs_sum, gs_in, *rest,
 ):
     early_bufs, late_bufs, rest = rest[:8], rest[8:16], rest[16:]
     own_sem, sa0, ra0, sa1, ra1, sl0, rl0, sl1, rl1, sc0, rc0, sc1, rc1, sg0, rg0, sg1, rg1 = rest[:17]
-    early_sems, late_sems, out_sems, known = rest[17:25], rest[25:33], rest[33], rest[34]
+    early_sems, late_sems, out_sems, known, load_sems = (
+        rest[17:25], rest[25:33], rest[33], rest[34], rest[35]
+    )
     blk = lax.axis_index("blk")
     scan = lax.axis_index("scan")
     chip = lax.div(blk, 2)
@@ -191,6 +193,9 @@
             send(src_all.at[origin], src_all.at[origin], (sa1, ra1), d, partner).start()
 
     plane = [{"scan": lax.rem(scan + d, PLANE)} for d in range(1, PLANE)]
+    pairs = ((wq_hbm, wq), (ref_hbm, ref), (wo_hbm, wo), (gout_hbm, gout), (wk_hbm, wk), (wv_hbm, wv))
+    loads = [pltpu.make_async_copy(a, b, load_sems.at[at]) for at, (a, b) in enumerate(pairs)]
+    own = pltpu.make_async_copy(src, src_all.at[blk], own_sem)
     barrier = pltpu.get_barrier_semaphore()
     row_at, col_at = lax.div(scan, 4), lax.rem(scan, 4)
     beside_z = [on_chip(1, core), on_chip(CHIPS - 1, core)]
@@ -207,6 +212,9 @@
 
     for target in everyone:
         pl.semaphore_signal(barrier, inc=1, device_id=target, device_id_type=MESH)
+    for load in loads:
+        load.start()
+    own.start()
 
     def all_reduce(bufs, sems):
         wg, w_swap, w_sum, w_in, w_part, z_all, w_row, w_all = bufs
@@ -269,6 +277,16 @@
 
         return swap[0].start, stage_1, stage_2, stage_3, stage_4, swap[1].wait_recv, left
 
+    pl.semaphore_wait(barrier, len(everyone))
+    for piece in range(PIECES):
+        for way in range(2):
+            ring_copy(blk, way, 1, piece, src).start()
+    send(src, src_all.at[blk], (sa1, ra1), 0, partner).start()
+    tell(0, beside_z)
+    tell(4, beside_x)
+
+    for load in loads:
+        load.wait()
     q_rows = nn(ref[...], wq[...]).astype(BF16)
     for head in range(HEADS):
         part = q_rows[:, group_cols(head)]
@@ -276,17 +294,6 @@
         qs[head] = jnp.where(own_lanes(ROWS, head), part, extra)
     qt_all[...] = q_rows.T
     rm[...] = jnp.full_like(rm, -3.0e38)
-    own = pltpu.make_async_copy(src, src_all.at[blk], own_sem)
-    own.start()
-
-    pl.semaphore_wait(barrier, len(everyone))
-    for piece in range(PIECES):
-        for way in range(2):
-            ring_copy(blk, way, 1, piece, src).start()
-    send(src, src_all.at[blk], (sa1, ra1), 0, partner).start()
-    tell(0, beside_z)
-    tell(4, beside_x)
-
     ga_rows = nt(gout[...], wo[...]).astype(BF16)
     gat_scr[...] = nt(wo[...], gout[...]).astype(BF16)
     for head in range(HEADS):
@@ -572,7 +579,7 @@
     pair = (TILES, 2, HEADS, BLOCK)
     columns = [vm(pair, F32), vm(pair, F32), vm(pair, F32), vm((TILES, CHIPS - 1, 2, HEADS, BLOCK), F32), vm(pair, F32)]
     scratch = [
-        vm((OUT_ROWS, D), BF16),
+        vm((ROWS, D), BF16), vm((ROWS, D), BF16), *[vm((D, D), BF16)] * 4, vm((OUT_ROWS, D), BF16),
         vm((2 * CHIPS, BLOCK, D), BF16), vm((TILES, D, TILE), BF16), vm((TILES, HEADS, TILE, BLOCK), BF16),
         vm((TILES, TILE, D), BF16), vm((TILES, D, TILE), BF16), vm(heads, BF16), vm(heads, BF16), vm(heads, BF16),
         vm(heads, BF16), vm((D, ROWS), BF16), vm((D, ROWS), BF16), vm((TILES, HEADS, ROWS, TILE), F32), vm(heads, F32), vm(heads, F32),
@@ -582,11 +589,11 @@
         vm((CHIPS - 1, D, BLOCK), BF16),
         *reduction, *reduction,
         DMA, DMA((8 * PIECES,)), DMA((8 * PIECES,)),
-    ] + [DMA((n,)) for n in (8,) * 14 + 2 * (2, 2, 15, 15, 7, 7, 15, 15) + (3,)] + [pltpu.SemaphoreType.REGULAR((7,))]
+    ] + [DMA((n,)) for n in (8,) * 14 + 2 * (2, 2, 15, 15, 7, 7, 15, 15) + (3,)] + [pltpu.SemaphoreType.REGULAR((7,)), DMA((6,))]
     return pl.pallas_call(
         layer_kernel,
         out_shape=shape((OUT_ROWS, D), BF16),
-        in_specs=[VMEM] * 7 + [SMEM],
+        in_specs=[HBM, HBM, VMEM, HBM, HBM, HBM, HBM, SMEM],
         out_specs=HBM,
         scratch_shapes=scratch,
         compiler_params=pltpu.CompilerParams(vmem_limit_bytes=60 << 20, collective_id=1, has_side_effects=True),

time: 84.6 us -> 84.3 us (level)
  no operation moved by 1% of the time
where the time goes in v8:
time: 84.3 us; the launch traced here: 84.1 us
  Pallas kernels  83.4 us (99%)
    pallas_call x1, Pallas kernels, layer(): pl.pallas_call(layer_kernel, out_shape=shape((OUT_ROWS, D), BF16), in_spe...  81.2 us
    pallas_call x1, Pallas kernels, finish(): pl.pallas_call(finish_kernel, out_shape=[shape((ROWS, D), BF16)] * 2 + [s...  2.28 us

profile of v8, /device:TPU:1, one launch (start us, length us, event | category | flops | bytes accessed | tf_op | source)
XLA Modules:
  0.0 84.1 jit_solution(6753429971029425621)
XLA Ops:
  0.6 81.2 %layer.1.parts = bf16[2176,256]{1,0:T(8,128)(2,1)} custom-call(bf16[512,256]{1,0:T(8,128)(2,1)} %bitcast.7, bf16[512,256]{1,0:T(8,128)(2,1)} %bitcast.8, bf16[128,256]{1,0:T(8,128)(2,1)} %bitcast.9, bf16[256,256]{1,0:T(8,128)(2,1)} %wq_hbm.1, bf16[256,256]{1,0:T(8,128)(2,1)} %wk_hbm.1, bf16[256,256]{1,0:T(8,128)(2,1)} %wv_hbm.1, bf16[256,256]{1,0:T(8,128)(2,1)} %wo_hbm.1, ...), custom_call_target="tpu_custom_call" | custom-call | tf_op jit(solution)/shard_map/layer/pallas_call | solution.py:593
  81.8 2.3 %finish.1 = (bf16[512,256]{1,0:T(8,128)(2,1)}, bf16[512,256]{1,0:T(8,128)(2,1)}, bf16[128,256]{1,0:T(8,128)(2,1)}, f32[256,256]{1,0:T(8,128)}, f32[256,256]{1,0:...) custom-call(bf16[2176,256]{1,0:T(8,128)(2,1)} %layer.1.parts), custom_call_target="tpu_custom_call" | custom-call | tf_op jit(solution)/shard_map/finish/pallas_call | solution.py:628
